TPU v7x, 128 devices: a whole 4x4x4 slice. The times are simulated.
128 devices in a mesh: py: 8 (over y, core), px: 16 (over z, x).
Axes of the slice: x: 4, y: 4, z: 4, core: 2. Of those that a mesh axis runs over, the one named last changes fastest.
Arguments:
- pieces: bfloat16 [8192, 128, 128], P(('py', 'px')), may hold values from -6 to 6
- owner_map: int32 [8192], P(('py', 'px')), may hold values from 0 to 127, as said below
- offsets: int32 [8192], P(('py', 'px')), may hold values from 0 to 63
- template: bfloat16 [8192, 16384], P('py', 'px'), may hold values from -32 to 32
- coefficients: float32 [3, 15], replicated, may hold values from -3 to 3
Outputs:
- difference: float32 [8192, 16384], P('py', 'px')
Inputs may be any that keep to these rules, and one draw needn't show every extreme that they name: owner_map[p] is the tile of the device holding p or one of the eight tiles around it inside the grid; no device sends more than 16 pieces to one tile, and every device sends exactly 16 to one of its tiles.
All inputs are finite; a program needn't handle non-finite values.
Results may differ from a plain program's by a relative error of at most 0.0021.
Values may be sent and summed in bfloat16 or wider, within the bound.
A program may use at most 128 MiB of HBM per device.

v0:
```python
import jax
import jax.numpy as jnp
from jax import lax
from jax.sharding import PartitionSpec as P

HALO = 16
CAP = 16


sigma_fractions = (0.09375, 0.1875, 0.375)
term_powers = [(degree - power_v, power_v) for degree in range(5) for power_v in range(degree + 1)]


def from_behind(array, axis, by):
    length = lax.axis_size(axis)
    pairs = [(i, i + by) for i in range(length) if 0 <= i + by < length]
    return lax.ppermute(array, axis, pairs)


def with_halo(block, sides, width):
    for axis, dim in sides:
        count = lax.axis_size(axis)
        forward = [(i, i + 1) for i in range(count - 1)]
        backward = [(target, source) for source, target in forward]
        low = lax.ppermute(
            lax.slice_in_dim(block, block.shape[dim] - width, None, axis=dim), axis, forward
        )
        high = lax.ppermute(lax.slice_in_dim(block, 0, width, axis=dim), axis, backward)
        block = jnp.concatenate([low, block, high], axis=dim)
    return block


def gauss_taps():
    positions = jnp.arange(-HALO, HALO + 1).astype(jnp.float32)
    stacked = []
    for fraction in sigma_fractions:
        sigma = fraction * HALO
        values = jnp.exp(-positions * positions / (2.0 * sigma * sigma))
        stacked.append(values / jnp.sum(values))
    return jnp.stack(stacked).astype(jnp.bfloat16)


def spatial_weight(coef_row, rows_coord, cols_coord):
    rows_pow = [jnp.ones_like(rows_coord)]
    cols_pow = [jnp.ones_like(cols_coord)]
    for degree in range(1, 5):
        rows_pow.append(rows_pow[-1] * rows_coord)
        cols_pow.append(cols_pow[-1] * cols_coord)
    running = jnp.zeros((rows_coord.shape[0], cols_coord.shape[0]), jnp.float32)
    for power_v in range(5):
        inner_sum = jnp.zeros_like(cols_coord)
        for power_u in range(5 - power_v):
            inner_sum = (
                inner_sum + coef_row[term_powers.index((power_u, power_v))] * cols_pow[power_u]
            )
        running = running + rows_pow[power_v][:, None] * inner_sum[None, :]
    return running


def banded(tap_row, out_count, widened):
    line = jnp.concatenate([tap_row, jnp.zeros((widened + 1 - tap_row.shape[0],), tap_row.dtype)])
    repeated = jnp.tile(line, out_count)[: out_count * widened]
    return repeated.reshape(out_count, widened)


def along_rows(piece_pair, offset_by):
    return from_behind((piece_pair[0], piece_pair[1]), "py", offset_by)


def along_cols(piece_pair, offset_by):
    return from_behind((piece_pair[0], piece_pair[1]), "px", offset_by)


def corner_rows(piece_pair, offset_by):
    return from_behind((piece_pair[0], piece_pair[1]), "py", offset_by)


def corner_cols(piece_pair, offset_by):
    return from_behind((piece_pair[0], piece_pair[1]), "px", offset_by)


def on_device(pieces, owner_map, offsets, template, coefficients):
    rows_total = lax.axis_size("py")
    cols_total = lax.axis_size("px")
    my_row = lax.axis_index("py")
    my_col = lax.axis_index("px")
    block_side = pieces.shape[1]
    tile_side = template.shape[0]
    blocks_side = tile_side // block_side
    step_row = owner_map // cols_total - my_row
    step_col = owner_map % cols_total - my_col
    bucket = 3 * (step_row + 1) + (step_col + 1)
    piece_order = jnp.arange(owner_map.shape[0], dtype=jnp.int32)
    earlier = (owner_map[:, None] == owner_map[None, :]) & (
        piece_order[:, None] > piece_order[None, :]
    )
    position = jnp.sum(earlier.astype(jnp.int32), axis=1)
    slot_index = bucket * CAP + position
    outgoing = jnp.zeros((9 * CAP, block_side, block_side), jnp.bfloat16).at[slot_index].set(pieces)
    outgoing = outgoing.reshape(3, 3, CAP, block_side, block_side)
    labels = jnp.zeros((9 * CAP,), jnp.int32).at[slot_index].set(offsets + 1).reshape(3, 3, CAP)
    collected = [(outgoing[1, 1], labels[1, 1])]
    collected.append(along_rows((outgoing[2, 1], labels[2, 1]), 1))
    collected.append(along_rows((outgoing[0, 1], labels[0, 1]), -1))
    collected.append(along_cols((outgoing[1, 2], labels[1, 2]), 1))
    collected.append(along_cols((outgoing[1, 0], labels[1, 0]), -1))
    for row_pick, col_pick in ((2, 2), (2, 0), (0, 2), (0, 0)):
        moved = corner_rows(
            (outgoing[row_pick, col_pick], labels[row_pick, col_pick]), row_pick - 1
        )
        collected.append(corner_cols((moved[0], moved[1]), col_pick - 1))
    slot_pieces = jnp.stack([entry[0] for entry in collected])
    slot_labels = jnp.stack([entry[1] for entry in collected])
    received = slot_pieces.reshape(-1, block_side * block_side)
    received_labels = slot_labels.reshape(-1)
    block_ids = jnp.arange(blocks_side * blocks_side, dtype=jnp.int32) + 1
    selector = received_labels[None, :] == block_ids[:, None]
    block_sums = jnp.dot(
        selector.astype(jnp.bfloat16), received, preferred_element_type=jnp.float32
    )
    coverage = jnp.sum(selector.astype(jnp.float32), axis=1)
    science = block_sums / jnp.maximum(coverage, 1.0)[:, None]
    science = (
        science.reshape(blocks_side, blocks_side, block_side, block_side)
        .transpose(0, 2, 1, 3)
        .reshape(tile_side, tile_side)
    )
    padded = with_halo(template, (("py", 0), ("px", 1)), HALO)
    widened = tile_side + 2 * HALO
    taps = gauss_taps()
    band_tables = [
        banded(taps[basis_index], tile_side, widened) for basis_index in range(len(sigma_fractions))
    ]
    stacked_bands = jnp.concatenate(band_tables, axis=0)
    across_all = lax.dot_general(
        padded, stacked_bands, (((1,), (1,)), ((), ())), preferred_element_type=jnp.float32
    ).astype(jnp.bfloat16)
    rows_coord = (
        (my_row * tile_side + jnp.arange(tile_side, dtype=jnp.int32)).astype(jnp.float32) + 0.5
    ) * (2.0 / (tile_side * rows_total)) - 1.0
    cols_coord = (
        (my_col * tile_side + jnp.arange(tile_side, dtype=jnp.int32)).astype(jnp.float32) + 0.5
    ) * (2.0 / (tile_side * cols_total)) - 1.0
    matched = jnp.zeros((tile_side, tile_side), jnp.float32)
    for basis_index in range(len(sigma_fractions)):
        across_part = across_all[:, basis_index * tile_side : (basis_index + 1) * tile_side]
        smoothed = jnp.dot(
            band_tables[basis_index], across_part, preferred_element_type=jnp.float32
        )
        matched = (
            matched + spatial_weight(coefficients[basis_index], rows_coord, cols_coord) * smoothed
        )
    return science - matched


def solution(mesh):
    in_specs = (P(("py", "px"), None, None), P(("py", "px")), P(("py", "px")), P("py", "px"), P())
    out_specs = P("py", "px")
    return jax.shard_map(
        on_device, mesh=mesh, in_specs=in_specs, out_specs=out_specs, check_vma=False
    )
```

profile of v0, /device:TPU:105, one launch (start us, length us, event | category | flops | bytes accessed | tf_op | source)
XLA Modules:
  0.0 242.8 jit_solution(320235680778076320)
XLA Ops:
  1.7 3.3 %broadcast_in_dim.8 = bf16[144,128,128]{2,1,0:T(8,128)(2,1)} broadcast(bf16[]{:T(256)} %constant.64.clone.1), dimensions={} | broadcast | bytes 4718594 | tf_op jit(solution)/shard_map/broadcast_in_dim | solution.py:99
  5.0 8.6 %scatter_fusion = bf16[144,128,128]{2,1,0:T(8,128)(2,1)} fusion(bf16[144,128,128]{2,1,0:T(8,128)(2,1)} %broadcast_in_dim.8, s32[64]{0:T(128)S(1)} %get-tuple-element.71, bf16[64,128,128]{2,1,0:T(8,128)(2,1)S(1)} %copy-done.3), kind=kCustom, calls=%fused_computation.1 | custom fusion | bytes 6291712 | tf_op jit(solution)/shard_map/scatter | solution.py:99
  13.7 4.1 %slice_bitcast_fusion = (bf16[16,128,128]{2,1,0:T(8,128)(2,1)S(1)}, bf16[16,128,128]{2,1,0:T(8,128)(2,1)}, bf16[16,128,128]{2,1,0:T(8,128)(2,1)}, bf16[16,128,12...) fusion(bf16[3,3,16,128,128]{4,3,2,1,0:T(8,128)(2,1)} %bitcast.130), kind=kLoop, calls=%fused_computation.18 | loop fusion | bytes 8388608 | tf_op jit(solution)/shard_map/squeeze | solution.py:109
  17.7 3.7 %collective-permute-start.12 = (bf16[16,128,128]{2,1,0:T(8,128)(2,1)}, bf16[16,128,128]{2,1,0:T(8,128)(2,1)}, u32[]{:S(2)}, u32[]{:S(2)}) collective-permute-start(bf16[16,128,128]{2,1,0:T(8,128)(2,1)} %get-tuple-element.12), channel_id=1, source_target_pairs={{0,16},{16,32},{32,48},{48,64},{64,80},{80,96},{96,112},{1,17},{17... | collective-permute-start | bytes 1572872 | tf_op jit(solution)/shard_map/ppermute | solution.py:17
  21.4 1.9 collective-permute-start.13
  23.4 3.1 %collective-permute-start.14 = (bf16[16,128,128]{2,1,0:T(8,128)(2,1)}, bf16[16,128,128]{2,1,0:T(8,128)(2,1)}, u32[]{:S(2)}, u32[]{:S(2)}) collective-permute-start(bf16[16,128,128]{2,1,0:T(8,128)(2,1)} %get-tuple-element.10), channel_id=1, source_target_pairs={{0,1},{1,2},{2,3},{3,4},{4,5},{5,6},{6,7},{7,8},{8,9},{9,10},{10,1... | collective-permute-start | bytes 1572872 | tf_op jit(solution)/shard_map/ppermute | solution.py:17
  27.4 3.9 %collective-permute-start = (s32[16]{0:T(128)S(1)}, s32[16]{0:T(128)S(1)}, u32[]{:S(2)}, u32[]{:S(2)}) collective-permute-start(s32[16]{0:T(128)S(1)} %get-tuple-element.24), channel_id=1, source_target_pairs={{0,16},{16,32},{32,48},{48,64},{64,80},{80,96},{96,112},{1,17},{17... | collective-permute-start | bytes 200 | tf_op jit(solution)/shard_map/ppermute | solution.py:17
  31.3 1.9 collective-permute-start.1
  40.1 4.5 %tile.30 = bf16[1082368]{0:T(1024)(128)(2,1)} reshape(bf16[1024,1057]{1,0:T(8,128)(2,1)S(1)} %tile.14) | data formatting | bytes 4329472 | tf_op jit(solution)/shard_map/tile | solution.py:62
  46.2 4.0 %reshape.288 = bf16[1024,1056]{1,0:T(8,128)(2,1)} reshape(bf16[1081344]{0:T(1024)(128)(2,1)S(1)} %slice-done) | data formatting | bytes 4325376 | tf_op jit(solution)/shard_map/reshape | solution.py:63
  51.8 4.5 %tile.32 = bf16[1082368]{0:T(1024)(128)(2,1)} reshape(bf16[1024,1057]{1,0:T(8,128)(2,1)S(1)} %tile.31) | data formatting | bytes 4329472 | tf_op jit(solution)/shard_map/tile | solution.py:62
  57.9 4.0 %reshape.289 = bf16[1024,1056]{1,0:T(8,128)(2,1)} reshape(bf16[1081344]{0:T(1024)(128)(2,1)S(1)} %slice-done.1) | data formatting | bytes 4325376 | tf_op jit(solution)/shard_map/reshape | solution.py:63
  62.9 4.5 %tile.13 = bf16[1082368]{0:T(1024)(128)(2,1)} reshape(bf16[1024,1057]{1,0:T(8,128)(2,1)S(1)} %tile.12) | data formatting | bytes 4329472 | tf_op jit(solution)/shard_map/tile | solution.py:62
  69.3 3.1 %multiply_add_fusion = (f32[1024]{0:T(1024)S(1)}, f32[1024]{0:T(1024)S(1)}) fusion(f32[]{:T(128)} %bitcast.83, f32[]{:T(128)} %bitcast.82, s32[]{:T(128)S(6)} %mul.731, f32[]{:T(128)} %bitcast.81, f32[]{:T(128)} %bitcast.80, f32[]{:T(128)} %bitcast.79), kind=kLoop, calls=%fused_computation.47 | loop fusion | flops 12288 | bytes 8216 | tf_op jit(solution)/shard_map/add | solution.py:54
  72.3 3.0 %multiply_add_fusion.4 = (f32[1024]{0:T(1024)S(1)}, f32[1024]{0:T(1024)S(1)}) fusion(f32[]{:T(128)} %bitcast.68, f32[]{:T(128)} %bitcast.67, s32[]{:T(128)S(6)} %mul.731, f32[]{:T(128)} %bitcast.66, f32[]{:T(128)} %bitcast.65, f32[]{:T(128)} %bitcast.64), kind=kLoop, calls=%fused_computation.51 | loop fusion | flops 12288 | bytes 8216 | tf_op jit(solution)/shard_map/add | solution.py:54
  75.4 3.3 %multiply_add_fusion.8 = (f32[1024]{0:T(1024)S(1)}, f32[1024]{0:T(1024)S(1)}) fusion(f32[]{:T(128)} %bitcast.50, f32[]{:T(128)} %bitcast.49, s32[]{:T(128)S(6)} %mul.731, f32[]{:T(128)} %bitcast.48, f32[]{:T(128)} %bitcast.47, f32[]{:T(128)} %bitcast.46), kind=kLoop, calls=%fused_computation.55 | loop fusion | flops 12288 | bytes 8216 | tf_op jit(solution)/shard_map/add | solution.py:54
  78.6 5.5 %multiply_add_fusion.2 = (f32[1024]{0:T(1024)S(1)}, f32[1024]{0:T(1024)S(1)}) fusion(f32[]{:T(128)} %bitcast.78, f32[]{:T(128)} %bitcast.77, f32[]{:T(128)} %bitcast.76, f32[]{:T(128)} %bitcast.75, s32[]{:T(128)S(6)} %mul.731, f32[]{:T(128)} %bitcast.74, f32[]{:T(128)} %bitcast.73, f32[]{:T(128)} %bitcast.72, f32[]{:T(128)} %bitcast.71, f32[]{:T(128)} %bitcast.70), kind=kLoop, calls=%fused_computation.49 | loop fusion | flops 22528 | bytes 8232 | tf_op jit(solution)/shard_map/add | solution.py:54
  84.2 5.7 %multiply_add_fusion.6 = (f32[1024]{0:T(1024)S(1)}, f32[1024]{0:T(1024)S(1)}) fusion(f32[]{:T(128)} %bitcast.63, f32[]{:T(128)} %bitcast.62, f32[]{:T(128)} %bitcast.61, f32[]{:T(128)} %bitcast.60, s32[]{:T(128)S(6)} %mul.731, f32[]{:T(128)} %bitcast.59, f32[]{:T(128)} %bitcast.58, f32[]{:T(128)} %bitcast.57, f32[]{:T(128)} %bitcast.56, f32[]{:T(128)} %bitcast.55), kind=kLoop, calls=%fused_computation.53 | loop fusion | flops 22528 | bytes 8232 | tf_op jit(solution)/shard_map/add | solution.py:54
  89.9 5.8 %multiply_add_fusion.10 = (f32[1024]{0:T(1024)S(1)}, f32[1024]{0:T(1024)S(1)}) fusion(f32[]{:T(128)} %bitcast.45, f32[]{:T(128)} %bitcast.44, f32[]{:T(128)} %bitcast.43, f32[]{:T(128)} %bitcast.42, s32[]{:T(128)S(6)} %mul.731, f32[]{:T(128)} %bitcast.41, f32[]{:T(128)} %bitcast.40, f32[]{:T(128)} %bitcast.39, f32[]{:T(128)} %bitcast.38, f32[]{:T(128)} %bitcast.37), kind=kLoop, calls=%fused_computation.57 | loop fusion | flops 22528 | bytes 8232 | tf_op jit(solution)/shard_map/add | solution.py:54
  95.7 4.1 %reshape.287 = bf16[1024,1056]{1,0:T(8,128)(2,1)} reshape(bf16[1081344]{0:T(1024)(128)(2,1)S(1)} %slice-done.2) | data formatting | bytes 4325376 | tf_op jit(solution)/shard_map/reshape | solution.py:63
  99.8 3.1 %collective-permute-start.2 = (s32[16]{0:T(128)S(1)}, s32[16]{0:T(128)S(1)}, u32[]{:S(2)}, u32[]{:S(2)}) collective-permute-start(s32[16]{0:T(128)S(1)} %get-tuple-element.22), channel_id=1, source_target_pairs={{0,1},{1,2},{2,3},{3,4},{4,5},{5,6},{6,7},{7,8},{8,9},{9,10},{10,1... | collective-permute-start | bytes 200 | tf_op jit(solution)/shard_map/ppermute | solution.py:17
  102.9 4.3 %collective-permute-start.3 = (s32[16]{0:T(128)S(1)}, s32[16]{0:T(128)S(1)}, u32[]{:S(2)}, u32[]{:S(2)}) collective-permute-start(s32[16]{0:T(128)S(1)} %get-tuple-element.21), channel_id=1, source_target_pairs={{1,0},{2,1},{3,2},{4,3},{5,4},{6,5},{7,6},{8,7},{9,8},{10,9},{11,1... | collective-permute-start | bytes 200 | tf_op jit(solution)/shard_map/ppermute | solution.py:17
  107.2 4.2 %collective-permute-start.4 = (s32[16]{0:T(128)S(1)}, s32[16]{0:T(128)S(1)}, u32[]{:S(2)}, u32[]{:S(2)}) collective-permute-start(s32[16]{0:T(128)S(1)} %get-tuple-element.20), channel_id=1, source_target_pairs={{0,16},{16,32},{32,48},{48,64},{64,80},{80,96},{96,112},{1,17},{17... | collective-permute-start | bytes 200 | tf_op jit(solution)/shard_map/ppermute | solution.py:17
  111.4 1.9 collective-permute-start.6
  113.3 2.4 collective-permute-start.8
  115.8 2.0 collective-permute-start.10
  120.6 5.0 %collective-permute-start.7 = (s32[16]{0:T(128)S(1)}, s32[16]{0:T(128)S(1)}, u32[]{:S(2)}, u32[]{:S(2)}) collective-permute-start(s32[16]{0:T(128)S(1)} %collective-permute-done.6), channel_id=1, source_target_pairs={{1,0},{2,1},{3,2},{4,3},{5,4},{6,5},{7,6},{8,7},{9,8},{10,9},{11,1... | collective-permute-start | bytes 200 | tf_op jit(solution)/shard_map/ppermute | solution.py:17
  127.6 5.5 %collective-permute-start.11 = (s32[16]{0:T(128)S(1)}, s32[16]{0:T(128)S(1)}, u32[]{:S(2)}, u32[]{:S(2)}) collective-permute-start(s32[16]{0:T(128)S(1)} %collective-permute-done.10), channel_id=1, source_target_pairs={{1,0},{2,1},{3,2},{4,3},{5,4},{6,5},{7,6},{8,7},{9,8},{10,9},{11,1... | collective-permute-start | bytes 200 | tf_op jit(solution)/shard_map/ppermute | solution.py:17
  133.1 4.3 %collective-permute-start.24 = (bf16[16,1024]{1,0:T(8,128)(2,1)S(1)}, bf16[16,1024]{1,0:T(8,128)(2,1)S(1)}, u32[]{:S(2)}, u32[]{:S(2)}) collective-permute-start(bf16[16,1024]{1,0:T(8,128)(2,1)S(1)} %get-tuple-element.16), channel_id=1, source_target_pairs={{0,16},{16,32},{32,48},{48,64},{64,80},{80,96},{96,112},{1,17},{17... | collective-permute-start | bytes 98312 | tf_op jit(solution)/shard_map/ppermute | solution.py:25
  142.8 1.9 collective-permute-start.26
  144.7 5.5 %collective-permute-start.27 = (bf16[1056,16]{1,0:T(8,128)(2,1)S(1)}, bf16[1056,16]{1,0:T(8,128)(2,1)}, u32[]{:S(2)}, u32[]{:S(2)}) collective-permute-start(bf16[1056,16]{1,0:T(8,128)(2,1)S(1)} %get-tuple-element.13), channel_id=1, source_target_pairs={{1,0},{2,1},{3,2},{4,3},{5,4},{6,5},{7,6},{8,7},{9,8},{10,9},{11,1... | collective-permute-start | bytes 101384 | tf_op jit(solution)/shard_map/ppermute | solution.py:28
  150.2 4.8 %collective-permute-done.26 = bf16[1056,16]{1,0:T(8,128)(2,1)} collective-permute-done((bf16[1056,16]{1,0:T(8,128)(2,1)S(1)}, bf16[1056,16]{1,0:T(8,128)(2,1)}, u32[]{:S(2)}, u32[]{:S(2)}) %collective-permute-start.26) | collective-permute-done | bytes 33824 | tf_op jit(solution)/shard_map/ppermute | solution.py:25
  155.0 3.6 %collective-permute-start.16 = (bf16[16,128,128]{2,1,0:T(8,128)(2,1)}, bf16[16,128,128]{2,1,0:T(8,128)(2,1)}, u32[]{:S(2)}, u32[]{:S(2)}) collective-permute-start(bf16[16,128,128]{2,1,0:T(8,128)(2,1)} %get-tuple-element.8), channel_id=1, source_target_pairs={{0,16},{16,32},{32,48},{48,64},{64,80},{80,96},{96,112},{1,17},{17... | collective-permute-start | bytes 1572872 | tf_op jit(solution)/shard_map/ppermute | solution.py:17
  158.6 1.9 collective-permute-start.18
  160.5 5.2 %concatenate.20 = bf16[1056,1056]{1,0:T(8,128)(2,1)} concatenate(bf16[1056,16]{1,0:T(8,128)(2,1)} %collective-permute-done.26, bf16[1056,1024]{1,0:T(8,128)(2,1)S(1)} %constant_dynamic-update-slice_fusion, bf16[1056,16]{1,0:T(8,128)(2,1)} %collective-permute-done.27), dimensions={1} | concatenate | bytes 4460544 | tf_op jit(solution)/shard_map/concatenate | solution.py:29
  165.7 14.0 %convolution_convert_fusion = bf16[1056,3072]{1,0:T(8,128)(2,1)} fusion(bf16[1056,1056]{1,0:T(8,128)(2,1)} %concatenate.20, bf16[1024,1056]{1,0:T(8,128)(2,1)} %reshape.289, bf16[1024,1056]{1,0:T(8,128)(2,1)} %reshape.288, bf16[1024,1056]{1,0:T(8,128)(2,1)} %reshape.287), kind=kOutput, calls=%fused_computation.3 | convolution fusion | flops 6874103808 | bytes 15206400 | tf_op jit(solution)/shard_map/dot_general | solution.py:135
  179.8 4.6 %fusion.11 = f32[1024,1024]{1,0:T(8,128)S(1)} fusion(bf16[1024,1056]{1,0:T(8,128)(2,1)S(1)} %copy-done.1, bf16[1056,3072]{1,0:T(8,128)(2,1)} %convolution_convert_fusion), kind=kOutput, calls=%fused_computation.14 | convolution fusion | flops 2214592512 | bytes 8519680 | tf_op jit(solution)/shard_map/dot_general | solution.py:147
  184.4 2.4 collective-permute-start.20
  186.9 2.2 collective-permute-start.22
  189.1 2.9 %fusion.13 = f32[1024,1024]{1,0:T(8,128)S(1)} fusion(bf16[1024,1056]{1,0:T(8,128)(2,1)S(1)} %copy-done.2, bf16[1056,3072]{1,0:T(8,128)(2,1)S(1)} %copy-done.6), kind=kOutput, calls=%fused_computation.16 | convolution fusion | flops 2214592512 | bytes 8716288 | tf_op jit(solution)/shard_map/dot_general | solution.py:147
  192.0 5.7 %collective-permute-start.15 = (bf16[16,128,128]{2,1,0:T(8,128)(2,1)S(1)}, bf16[16,128,128]{2,1,0:T(8,128)(2,1)S(1)}, u32[]{:S(2)}, u32[]{:S(2)}) collective-permute-start(bf16[16,128,128]{2,1,0:T(8,128)(2,1)S(1)} %get-tuple-element.9), channel_id=1, source_target_pairs={{1,0},{2,1},{3,2},{4,3},{5,4},{6,5},{7,6},{8,7},{9,8},{10,9},{11,1... | collective-permute-start | bytes 1572872 | tf_op jit(solution)/shard_map/ppermute | solution.py:17
  202.0 5.5 %collective-permute-start.19 = (bf16[16,128,128]{2,1,0:T(8,128)(2,1)}, bf16[16,128,128]{2,1,0:T(8,128)(2,1)S(1)}, u32[]{:S(2)}, u32[]{:S(2)}) collective-permute-start(bf16[16,128,128]{2,1,0:T(8,128)(2,1)} %collective-permute-done.18), channel_id=1, source_target_pairs={{1,0},{2,1},{3,2},{4,3},{5,4},{6,5},{7,6},{8,7},{9,8},{10,9},{11,1... | collective-permute-start | bytes 1572872 | tf_op jit(solution)/shard_map/ppermute | solution.py:17
  209.4 5.7 %collective-permute-start.23 = (bf16[16,128,128]{2,1,0:T(8,128)(2,1)S(1)}, bf16[16,128,128]{2,1,0:T(8,128)(2,1)S(1)}, u32[]{:S(2)}, u32[]{:S(2)}) collective-permute-start(bf16[16,128,128]{2,1,0:T(8,128)(2,1)S(1)} %collective-permute-done.22), channel_id=1, source_target_pairs={{1,0},{2,1},{3,2},{4,3},{5,4},{6,5},{7,6},{8,7},{9,8},{10,9},{11,1... | collective-permute-start | bytes 1572872 | tf_op jit(solution)/shard_map/ppermute | solution.py:17
  216.5 4.0 %collective-permute-done.19 = bf16[16,128,128]{2,1,0:T(8,128)(2,1)S(1)} collective-permute-done((bf16[16,128,128]{2,1,0:T(8,128)(2,1)}, bf16[16,128,128]{2,1,0:T(8,128)(2,1)S(1)}, u32[]{:S(2)}, u32[]{:S(2)}) %collective-permute-start.19) | collective-permute-done | bytes 524320 | tf_op jit(solution)/shard_map/ppermute | solution.py:17
  220.5 7.1 %collective-permute-done.21 = bf16[16,128,128]{2,1,0:T(8,128)(2,1)S(1)} collective-permute-done((bf16[16,128,128]{2,1,0:T(8,128)(2,1)S(1)}, bf16[16,128,128]{2,1,0:T(8,128)(2,1)S(1)}, u32[]{:S(2)}, u32[]{:S(2)}) %collective-permute-start.21) | collective-permute-done | bytes 524320 | tf_op jit(solution)/shard_map/ppermute | solution.py:17
  227.7 3.9 %collective-permute-done.23 = bf16[16,128,128]{2,1,0:T(8,128)(2,1)S(1)} collective-permute-done((bf16[16,128,128]{2,1,0:T(8,128)(2,1)S(1)}, bf16[16,128,128]{2,1,0:T(8,128)(2,1)S(1)}, u32[]{:S(2)}, u32[]{:S(2)}) %collective-permute-start.23) | collective-permute-done | bytes 524320 | tf_op jit(solution)/shard_map/ppermute | solution.py:17
  231.7 3.2 %convolution_divide_fusion = f32[64,16384]{1,0:T(8,128)S(1)} fusion(bf16[18,8,128,128]{3,2,1,0:T(8,128)(2,1)S(1)} %bitcast.134, f32[64]{0:T(128)S(1)} %broadcast_maximum_fusion, s32[144]{0:T(256)S(1)} %eq.33, s32[64]{0:T(128)S(1)} %iota_add_fusion), kind=kOutput, calls=%fused_computation.2 | convolution fusion | flops 303047680 | bytes 8913984 | tf_op jit(solution)/shard_map/dot_general | solution.py:118
  234.8 7.9 %bitcast_subtract_fusion = f32[1024,1024]{1,0:T(8,128)} fusion(f32[128,8,8,128]{3,2,1,0:T(8,128)S(1)} %bitcast.143, f32[1024,1024]{1,0:T(8,128)S(1)} %fusion.11, f32[1024,1024]{1,0:T(8,128)S(1)} %fusion.13, bf16[1024,1056]{1,0:T(8,128)(2,1)S(1)} %copy-done, bf16[1056,3072]{1,0:T(8,128)(2,1)S(1)} %copy-done.6, f32[1024]{0:T(1024)S(1)} %get-tuple-element.76, ...), kind=kOutput, calls=%fused_computation.11 | convolution fusion | flops 2242904064 | bytes 21372928 | tf_op jit(solution)/shard_map/dot_general | solution.py:147
  (96 shorter events, 34.9 us)
Async XLA Ops:
  0.0 5.0 %copy-start.3 = (bf16[64,128,128]{2,1,0:T(8,128)(2,1)S(1)}, bf16[64,128,128]{2,1,0:T(8,128)(2,1)}, u32[]{:S(2)}) copy-start(bf16[64,128,128]{2,1,0:T(8,128)(2,1)} %param.5) | copy-start | bytes 6291460
  13.7 23.4 %copy-start.5 = (f32[3,15]{1,0:T(4,128)S(1)}, f32[3,15]{1,0:T(4,128)}, u32[]{:S(2)}) copy-start(f32[3,15]{1,0:T(4,128)} %param.9) | copy-start | bytes 544
  17.7 166.7 %collective-permute-start.12 = (bf16[16,128,128]{2,1,0:T(8,128)(2,1)}, bf16[16,128,128]{2,1,0:T(8,128)(2,1)}, u32[]{:S(2)}, u32[]{:S(2)}) collective-permute-start(bf16[16,128,128]{2,1,0:T(8,128)(2,1)} %get-tuple-element.12), channel_id=1, source_target_pairs={{0,16},{16,32},{32,48},{48,64},{64,80},{80,96},{96,112},{1,17},{17... | collective-permute-start | bytes 1572872 | tf_op jit(solution)/shard_map/ppermute | solution.py:17
  21.4 165.4 %collective-permute-start.13 = (bf16[16,128,128]{2,1,0:T(8,128)(2,1)}, bf16[16,128,128]{2,1,0:T(8,128)(2,1)}, u32[]{:S(2)}, u32[]{:S(2)}) collective-permute-start(bf16[16,128,128]{2,1,0:T(8,128)(2,1)} %get-tuple-element.11), channel_id=1, source_target_pairs={{16,0},{32,16},{48,32},{64,48},{80,64},{96,80},{112,96},{17,1},{33... | collective-permute-start | bytes 1572872 | tf_op jit(solution)/shard_map/ppermute | solution.py:17
  23.4 168.6 %collective-permute-start.14 = (bf16[16,128,128]{2,1,0:T(8,128)(2,1)}, bf16[16,128,128]{2,1,0:T(8,128)(2,1)}, u32[]{:S(2)}, u32[]{:S(2)}) collective-permute-start(bf16[16,128,128]{2,1,0:T(8,128)(2,1)} %get-tuple-element.10), channel_id=1, source_target_pairs={{0,1},{1,2},{2,3},{3,4},{4,5},{5,6},{6,7},{7,8},{8,9},{9,10},{10,1... | collective-permute-start | bytes 1572872 | tf_op jit(solution)/shard_map/ppermute | solution.py:17
  27.4 72.4 %collective-permute-start = (s32[16]{0:T(128)S(1)}, s32[16]{0:T(128)S(1)}, u32[]{:S(2)}, u32[]{:S(2)}) collective-permute-start(s32[16]{0:T(128)S(1)} %get-tuple-element.24), channel_id=1, source_target_pairs={{0,16},{16,32},{32,48},{48,64},{64,80},{80,96},{96,112},{1,17},{17... | collective-permute-start | bytes 200 | tf_op jit(solution)/shard_map/ppermute | solution.py:17
  31.3 71.6 %collective-permute-start.1 = (s32[16]{0:T(128)S(1)}, s32[16]{0:T(128)S(1)}, u32[]{:S(2)}, u32[]{:S(2)}) collective-permute-start(s32[16]{0:T(128)S(1)} %get-tuple-element.23), channel_id=1, source_target_pairs={{16,0},{32,16},{48,32},{64,48},{80,64},{96,80},{112,96},{17,1},{33... | collective-permute-start | bytes 200 | tf_op jit(solution)/shard_map/ppermute | solution.py:17
  44.6 1.6 slice-start
  56.3 1.6 slice-start.1
  67.3 28.3 %slice-start.2 = ((bf16[1082368]{0:T(1024)(128)(2,1)}), bf16[1081344]{0:T(1024)(128)(2,1)S(1)}, s32[]{:S(2)}) async-start(bf16[1082368]{0:T(1024)(128)(2,1)} %tile.13), calls=%async_computation.2 | async-start | bytes 4325376 | tf_op jit(solution)/shard_map/slice | solution.py:62
  99.8 7.4 %collective-permute-start.2 = (s32[16]{0:T(128)S(1)}, s32[16]{0:T(128)S(1)}, u32[]{:S(2)}, u32[]{:S(2)}) collective-permute-start(s32[16]{0:T(128)S(1)} %get-tuple-element.22), channel_id=1, source_target_pairs={{0,1},{1,2},{2,3},{3,4},{4,5},{5,6},{6,7},{7,8},{8,9},{9,10},{10,1... | collective-permute-start | bytes 200 | tf_op jit(solution)/shard_map/ppermute | solution.py:17
  102.9 8.5 %collective-permute-start.3 = (s32[16]{0:T(128)S(1)}, s32[16]{0:T(128)S(1)}, u32[]{:S(2)}, u32[]{:S(2)}) collective-permute-start(s32[16]{0:T(128)S(1)} %get-tuple-element.21), channel_id=1, source_target_pairs={{1,0},{2,1},{3,2},{4,3},{5,4},{6,5},{7,6},{8,7},{9,8},{10,9},{11,1... | collective-permute-start | bytes 200 | tf_op jit(solution)/shard_map/ppermute | solution.py:17
  107.2 6.2 %collective-permute-start.4 = (s32[16]{0:T(128)S(1)}, s32[16]{0:T(128)S(1)}, u32[]{:S(2)}, u32[]{:S(2)}) collective-permute-start(s32[16]{0:T(128)S(1)} %get-tuple-element.20), channel_id=1, source_target_pairs={{0,16},{16,32},{32,48},{48,64},{64,80},{80,96},{96,112},{1,17},{17... | collective-permute-start | bytes 200 | tf_op jit(solution)/shard_map/ppermute | solution.py:17
  111.4 4.4 %collective-permute-start.6 = (s32[16]{0:T(128)S(1)}, s32[16]{0:T(128)S(1)}, u32[]{:S(2)}, u32[]{:S(2)}) collective-permute-start(s32[16]{0:T(128)S(1)} %get-tuple-element.19), channel_id=1, source_target_pairs={{0,16},{16,32},{32,48},{48,64},{64,80},{80,96},{96,112},{1,17},{17... | collective-permute-start | bytes 200 | tf_op jit(solution)/shard_map/ppermute | solution.py:17
  113.3 4.9 %collective-permute-start.8 = (s32[16]{0:T(128)S(1)}, s32[16]{0:T(128)S(1)}, u32[]{:S(2)}, u32[]{:S(2)}) collective-permute-start(s32[16]{0:T(128)S(1)} %get-tuple-element.18), channel_id=1, source_target_pairs={{16,0},{32,16},{48,32},{64,48},{80,64},{96,80},{112,96},{17,1},{33... | collective-permute-start | bytes 200 | tf_op jit(solution)/shard_map/ppermute | solution.py:17
  115.8 4.9 %collective-permute-start.10 = (s32[16]{0:T(128)S(1)}, s32[16]{0:T(128)S(1)}, u32[]{:S(2)}, u32[]{:S(2)}) collective-permute-start(s32[16]{0:T(128)S(1)} %get-tuple-element.17), channel_id=1, source_target_pairs={{16,0},{32,16},{48,32},{64,48},{80,64},{96,80},{112,96},{17,1},{33... | collective-permute-start | bytes 200 | tf_op jit(solution)/shard_map/ppermute | solution.py:17
  118.2 7.4 %collective-permute-start.5 = (s32[16]{0:T(128)S(1)}, s32[16]{0:T(128)S(1)}, u32[]{:S(2)}, u32[]{:S(2)}) collective-permute-start(s32[16]{0:T(128)S(1)} %collective-permute-done.4), channel_id=1, source_target_pairs={{0,1},{1,2},{2,3},{3,4},{4,5},{5,6},{6,7},{7,8},{8,9},{9,10},{10,1... | collective-permute-start | bytes 200 | tf_op jit(solution)/shard_map/ppermute | solution.py:17
  120.6 6.9 %collective-permute-start.7 = (s32[16]{0:T(128)S(1)}, s32[16]{0:T(128)S(1)}, u32[]{:S(2)}, u32[]{:S(2)}) collective-permute-start(s32[16]{0:T(128)S(1)} %collective-permute-done.6), channel_id=1, source_target_pairs={{1,0},{2,1},{3,2},{4,3},{5,4},{6,5},{7,6},{8,7},{9,8},{10,9},{11,1... | collective-permute-start | bytes 200 | tf_op jit(solution)/shard_map/ppermute | solution.py:17
  125.6 7.4 %collective-permute-start.9 = (s32[16]{0:T(128)S(1)}, s32[16]{0:T(128)S(1)}, u32[]{:S(2)}, u32[]{:S(2)}) collective-permute-start(s32[16]{0:T(128)S(1)} %collective-permute-done.8), channel_id=1, source_target_pairs={{0,1},{1,2},{2,3},{3,4},{4,5},{5,6},{6,7},{7,8},{8,9},{9,10},{10,1... | collective-permute-start | bytes 200 | tf_op jit(solution)/shard_map/ppermute | solution.py:17
  127.6 9.8 %collective-permute-start.11 = (s32[16]{0:T(128)S(1)}, s32[16]{0:T(128)S(1)}, u32[]{:S(2)}, u32[]{:S(2)}) collective-permute-start(s32[16]{0:T(128)S(1)} %collective-permute-done.10), channel_id=1, source_target_pairs={{1,0},{2,1},{3,2},{4,3},{5,4},{6,5},{7,6},{8,7},{9,8},{10,9},{11,1... | collective-permute-start | bytes 200 | tf_op jit(solution)/shard_map/ppermute | solution.py:17
  133.1 6.5 %collective-permute-start.24 = (bf16[16,1024]{1,0:T(8,128)(2,1)S(1)}, bf16[16,1024]{1,0:T(8,128)(2,1)S(1)}, u32[]{:S(2)}, u32[]{:S(2)}) collective-permute-start(bf16[16,1024]{1,0:T(8,128)(2,1)S(1)} %get-tuple-element.16), channel_id=1, source_target_pairs={{0,16},{16,32},{32,48},{48,64},{64,80},{80,96},{96,112},{1,17},{17... | collective-permute-start | bytes 98312 | tf_op jit(solution)/shard_map/ppermute | solution.py:25
  137.3 5.2 %collective-permute-start.25 = (bf16[16,1024]{1,0:T(8,128)(2,1)S(1)}, bf16[16,1024]{1,0:T(8,128)(2,1)S(1)}, u32[]{:S(2)}, u32[]{:S(2)}) collective-permute-start(bf16[16,1024]{1,0:T(8,128)(2,1)S(1)} %get-tuple-element.15), channel_id=1, source_target_pairs={{16,0},{32,16},{48,32},{64,48},{80,64},{96,80},{112,96},{17,1},{33... | collective-permute-start | bytes 98312 | tf_op jit(solution)/shard_map/ppermute | solution.py:28
  142.8 12.2 %collective-permute-start.26 = (bf16[1056,16]{1,0:T(8,128)(2,1)S(1)}, bf16[1056,16]{1,0:T(8,128)(2,1)}, u32[]{:S(2)}, u32[]{:S(2)}) collective-permute-start(bf16[1056,16]{1,0:T(8,128)(2,1)S(1)} %get-tuple-element.14), channel_id=1, source_target_pairs={{0,1},{1,2},{2,3},{3,4},{4,5},{5,6},{6,7},{7,8},{8,9},{9,10},{10,1... | collective-permute-start | bytes 101384 | tf_op jit(solution)/shard_map/ppermute | solution.py:25
  144.7 13.9 %collective-permute-start.27 = (bf16[1056,16]{1,0:T(8,128)(2,1)S(1)}, bf16[1056,16]{1,0:T(8,128)(2,1)}, u32[]{:S(2)}, u32[]{:S(2)}) collective-permute-start(bf16[1056,16]{1,0:T(8,128)(2,1)S(1)} %get-tuple-element.13), channel_id=1, source_target_pairs={{1,0},{2,1},{3,2},{4,3},{5,4},{6,5},{7,6},{8,7},{9,8},{10,9},{11,1... | collective-permute-start | bytes 101384 | tf_op jit(solution)/shard_map/ppermute | solution.py:28
  155.0 43.9 %collective-permute-start.16 = (bf16[16,128,128]{2,1,0:T(8,128)(2,1)}, bf16[16,128,128]{2,1,0:T(8,128)(2,1)}, u32[]{:S(2)}, u32[]{:S(2)}) collective-permute-start(bf16[16,128,128]{2,1,0:T(8,128)(2,1)} %get-tuple-element.8), channel_id=1, source_target_pairs={{0,16},{16,32},{32,48},{48,64},{64,80},{80,96},{96,112},{1,17},{17... | collective-permute-start | bytes 1572872 | tf_op jit(solution)/shard_map/ppermute | solution.py:17
  158.6 43.4 %collective-permute-start.18 = (bf16[16,128,128]{2,1,0:T(8,128)(2,1)}, bf16[16,128,128]{2,1,0:T(8,128)(2,1)}, u32[]{:S(2)}, u32[]{:S(2)}) collective-permute-start(bf16[16,128,128]{2,1,0:T(8,128)(2,1)} %get-tuple-element.7), channel_id=1, source_target_pairs={{0,16},{16,32},{32,48},{48,64},{64,80},{80,96},{96,112},{1,17},{17... | collective-permute-start | bytes 1572872 | tf_op jit(solution)/shard_map/ppermute | solution.py:17
  165.7 14.0 %copy-start.1 = (bf16[1024,1056]{1,0:T(8,128)(2,1)S(1)}, bf16[1024,1056]{1,0:T(8,128)(2,1)}, u32[]{:S(2)}) copy-start(bf16[1024,1056]{1,0:T(8,128)(2,1)} %reshape.288) | copy-start | bytes 6488068
  179.7 4.7 %copy-start.4 = (bf16[16,128,128]{2,1,0:T(8,128)(2,1)S(1)}, bf16[16,128,128]{2,1,0:T(8,128)(2,1)}, u32[]{:S(2)}) copy-start(bf16[16,128,128]{2,1,0:T(8,128)(2,1)} %get-tuple-element.6) | copy-start | bytes 1572868
  179.7 9.4 %copy-start.2 = (bf16[1024,1056]{1,0:T(8,128)(2,1)S(1)}, bf16[1024,1056]{1,0:T(8,128)(2,1)}, u32[]{:S(2)}) copy-start(bf16[1024,1056]{1,0:T(8,128)(2,1)} %reshape.287) | copy-start | bytes 6488068
  179.7 9.4 %copy-start.6 = (bf16[1056,3072]{1,0:T(8,128)(2,1)S(1)}, bf16[1056,3072]{1,0:T(8,128)(2,1)}, u32[]{:S(2)}) copy-start(bf16[1056,3072]{1,0:T(8,128)(2,1)} %convolution_convert_fusion) | copy-start | bytes 19464196
  184.4 23.1 %collective-permute-start.20 = (bf16[16,128,128]{2,1,0:T(8,128)(2,1)S(1)}, bf16[16,128,128]{2,1,0:T(8,128)(2,1)S(1)}, u32[]{:S(2)}, u32[]{:S(2)}) collective-permute-start(bf16[16,128,128]{2,1,0:T(8,128)(2,1)S(1)} %copy-done.4), channel_id=1, source_target_pairs={{16,0},{32,16},{48,32},{64,48},{80,64},{96,80},{112,96},{17,1},{33... | collective-permute-start | bytes 1572872 | tf_op jit(solution)/shard_map/ppermute | solution.py:17
  186.8 10.9 %slice-start.3 = ((s8[4718592]{0:T(1024)(128)(4,1)}), s8[4194304]{0:T(1024)(128)(4,1)S(1)}, s32[]{:S(2)}) async-start(s8[4718592]{0:T(1024)(128)(4,1)} %bitcast.132), calls=%async_computation.3 | async-start | bytes 8388608
  186.8 10.9 %slice-start.4 = ((s8[4718592]{0:T(1024)(128)(4,1)}), s8[524288]{0:T(1024)(128)(4,1)S(1)}, s32[]{:S(2)}) async-start(s8[4718592]{0:T(1024)(128)(4,1)} %bitcast.132), calls=%async_computation.4 | async-start | bytes 1048576
  186.9 22.6 %collective-permute-start.22 = (bf16[16,128,128]{2,1,0:T(8,128)(2,1)S(1)}, bf16[16,128,128]{2,1,0:T(8,128)(2,1)S(1)}, u32[]{:S(2)}, u32[]{:S(2)}) collective-permute-start(bf16[16,128,128]{2,1,0:T(8,128)(2,1)S(1)} %get-tuple-element.5), channel_id=1, source_target_pairs={{16,0},{32,16},{48,32},{64,48},{80,64},{96,80},{112,96},{17,1},{33... | collective-permute-start | bytes 1572872 | tf_op jit(solution)/shard_map/ppermute | solution.py:17
  192.0 24.2 %collective-permute-start.15 = (bf16[16,128,128]{2,1,0:T(8,128)(2,1)S(1)}, bf16[16,128,128]{2,1,0:T(8,128)(2,1)S(1)}, u32[]{:S(2)}, u32[]{:S(2)}) collective-permute-start(bf16[16,128,128]{2,1,0:T(8,128)(2,1)S(1)} %get-tuple-element.9), channel_id=1, source_target_pairs={{1,0},{2,1},{3,2},{4,3},{5,4},{6,5},{7,6},{8,7},{9,8},{10,9},{11,1... | collective-permute-start | bytes 1572872 | tf_op jit(solution)/shard_map/ppermute | solution.py:17
  198.9 17.4 %collective-permute-start.17 = (bf16[16,128,128]{2,1,0:T(8,128)(2,1)}, bf16[16,128,128]{2,1,0:T(8,128)(2,1)S(1)}, u32[]{:S(2)}, u32[]{:S(2)}) collective-permute-start(bf16[16,128,128]{2,1,0:T(8,128)(2,1)} %collective-permute-done.16), channel_id=1, source_target_pairs={{0,1},{1,2},{2,3},{3,4},{4,5},{5,6},{6,7},{7,8},{8,9},{9,10},{10,1... | collective-permute-start | bytes 1572872 | tf_op jit(solution)/shard_map/ppermute | solution.py:17
  202.0 18.4 %collective-permute-start.19 = (bf16[16,128,128]{2,1,0:T(8,128)(2,1)}, bf16[16,128,128]{2,1,0:T(8,128)(2,1)S(1)}, u32[]{:S(2)}, u32[]{:S(2)}) collective-permute-start(bf16[16,128,128]{2,1,0:T(8,128)(2,1)} %collective-permute-done.18), channel_id=1, source_target_pairs={{1,0},{2,1},{3,2},{4,3},{5,4},{6,5},{7,6},{8,7},{9,8},{10,9},{11,1... | collective-permute-start | bytes 1572872 | tf_op jit(solution)/shard_map/ppermute | solution.py:17
  207.5 20.1 %collective-permute-start.21 = (bf16[16,128,128]{2,1,0:T(8,128)(2,1)S(1)}, bf16[16,128,128]{2,1,0:T(8,128)(2,1)S(1)}, u32[]{:S(2)}, u32[]{:S(2)}) collective-permute-start(bf16[16,128,128]{2,1,0:T(8,128)(2,1)S(1)} %collective-permute-done.20), channel_id=1, source_target_pairs={{0,1},{1,2},{2,3},{3,4},{4,5},{5,6},{6,7},{7,8},{8,9},{9,10},{10,1... | collective-permute-start | bytes 1572872 | tf_op jit(solution)/shard_map/ppermute | solution.py:17
  209.4 22.1 %collective-permute-start.23 = (bf16[16,128,128]{2,1,0:T(8,128)(2,1)S(1)}, bf16[16,128,128]{2,1,0:T(8,128)(2,1)S(1)}, u32[]{:S(2)}, u32[]{:S(2)}) collective-permute-start(bf16[16,128,128]{2,1,0:T(8,128)(2,1)S(1)} %collective-permute-done.22), channel_id=1, source_target_pairs={{1,0},{2,1},{3,2},{4,3},{5,4},{6,5},{7,6},{8,7},{9,8},{10,9},{11,1... | collective-permute-start | bytes 1572872 | tf_op jit(solution)/shard_map/ppermute | solution.py:17
  231.6 3.2 %copy-start = (bf16[1024,1056]{1,0:T(8,128)(2,1)S(1)}, bf16[1024,1056]{1,0:T(8,128)(2,1)}, u32[]{:S(2)}) copy-start(bf16[1024,1056]{1,0:T(8,128)(2,1)} %reshape.289) | copy-start | bytes 6488068
where the time goes:
time: 248 us; the launch traced here: 243 us
  starting transfers between devices  91.2 us (37%)
  local copies, waits for them, and re-layouts  62 us (25%)
  other arithmetic  34.2 us (14%)
  matrix products  32.7 us (13%)
  waiting for transfers between devices  22 us (9%)
    ppermute x24, starting transfers between devices, from_behind(): return lax.ppermute(array, axis, pairs)  77.6 us
    add x6, other arithmetic, spatial_weight(): inner_sum + coef_row[term_powers.index((power_u, power_v))] * cols_pow[po...  26.4 us
    ppermute x24, waiting for transfers between devices, from_behind(): return lax.ppermute(array, axis, pairs)  16 us
    dot_general x3, matrix products, on_device(): jnp.dot(band_tables[basis_index], across_part, preferred_element_type=jnp...  15.5 us
    dot_general x1, matrix products, on_device(): lax.dot_general(padded, stacked_bands, (((1,), (1,)), ((), ())), preferre...  14 us
    another operation x6, local copies, waits for them, and re-layouts, banded(): repeated = jnp.tile(line, out_count)[:out_count * widened]  14 us
    reshape x3, local copies, waits for them, and re-layouts, banded(): return repeated.reshape(out_count, widened)  12.2 us
    scatter x1, local copies, waits for them, and re-layouts, on_device(): jnp.zeros((9 * CAP, block_side, block_side), jnp.bfloat16).at[slot_index]  8.64 us
  transfers between devices with their start and end apart: 28, of which 7 were waited for; matrix products, arithmetic and copies ran while one was open for 40% of the time, Pallas kernels for 0%

commit v1 on v0

v1 whole, which is shorter than its diff:
```python
import functools

import jax
import jax.numpy as jnp
import numpy as np
from jax import lax
from jax.experimental import pallas as pl
from jax.experimental.pallas import tpu as pltpu
from jax.sharding import PartitionSpec as P

HALO = 16
CAP = 16
LANES = 128
BASES = 3
DEGREE = 4

sigma_fractions = (0.09375, 0.1875, 0.375)
term_powers = [(degree - power_v, power_v) for degree in range(5) for power_v in range(degree + 1)]

DIRS = ((0, 1), (0, -1), (1, 1), (1, -1), (-1, 1), (-1, -1), (1, 0), (-1, 0))
OWN = 4
MESH = pl.DeviceIdType.MESH


def bucket_of(step):
    return 3 * (step[0] + 1) + step[1] + 1


def gauss_taps():
    positions = np.arange(-HALO, HALO + 1).astype(np.float32)
    stacked = []
    for fraction in sigma_fractions:
        sigma = fraction * HALO
        values = np.exp(-positions * positions / np.float32(2.0 * sigma * sigma))
        stacked.append(values / np.sum(values))
    return np.stack(stacked).astype(jnp.bfloat16)


def band_tables():
    taps = gauss_taps()
    across = np.zeros((3 * LANES, BASES * LANES), taps.dtype)
    down = np.zeros((BASES, LANES, 2 * LANES), taps.dtype)
    for basis in range(BASES):
        for out in range(LANES):
            for tap in range(2 * HALO + 1):
                across[LANES - HALO + out + tap, basis * LANES + out] = taps[basis, tap]
                down[basis, out, out + tap] = taps[basis, tap]
    return across, down


def slots_kernel(owner, offset, index, label, count):
    row, col = lax.axis_index("py"), lax.axis_index("px")
    cols = lax.axis_size("px")
    for bucket in range(9):
        count[bucket] = 0

    def clear(slot, carry):
        for bucket in range(9):
            index[bucket, slot] = 0
            label[bucket, slot] = 0
        return carry

    lax.fori_loop(0, CAP, clear, 0)

    def place(piece, carry):
        tile = owner[piece]
        bucket = 3 * (lax.div(tile, cols) - row + 1) + lax.rem(tile, cols) - col + 1
        slot = count[bucket]
        count[bucket] = slot + 1
        index[bucket, slot] = piece
        label[bucket, slot] = offset[piece] + 1
        return carry

    lax.fori_loop(0, owner.shape[0], place, 0)


def send_kernel(
    index, coef, label, pieces, template, band_across, band_down,
    arrived, arrived_label, matched,
    held, outgoing, padded, strip_out, strip_in, across, inner, result,
    load_sem, send_sem, recv_sem, label_send, label_recv, rim_send, rim_recv, out_sem,
):
    rows, cols = lax.axis_size("py"), lax.axis_size("px")
    row, col = lax.axis_index("py"), lax.axis_index("px")
    side = template.shape[0]
    last = side - LANES

    def exists(step):
        r, c = row + step[0], col + step[1]
        return (r >= 0) & (r < rows) & (c >= 0) & (c < cols)

    def neighbour(step):
        return (row + step[0], col + step[1])

    body = padded.at[pl.ds(HALO, side)]
    loads = [
        pltpu.make_async_copy(template.at[:, pl.ds(0, LANES)], body.at[:, pl.ds(LANES, LANES)], load_sem.at[0]),
        pltpu.make_async_copy(template.at[:, pl.ds(last, LANES)], body.at[:, pl.ds(side, LANES)], load_sem.at[1]),
        pltpu.make_async_copy(pieces, held, load_sem.at[2]),
        pltpu.make_async_copy(
            template.at[:, pl.ds(LANES, side - 2 * LANES)],
            body.at[:, pl.ds(2 * LANES, side - 2 * LANES)],
            load_sem.at[3],
        ),
    ]
    for load in loads:
        load.start()

    barrier = pltpu.get_barrier_semaphore()
    for step in DIRS:
        @pl.when(exists(step))
        def _():
            pl.semaphore_signal(barrier, inc=1, device_id=neighbour(step), device_id_type=MESH)
    tall_group = 3 - jnp.where(row == 0, 1, 0) - jnp.where(row == rows - 1, 1, 0)
    wide_group = 3 - jnp.where(col == 0, 1, 0) - jnp.where(col == cols - 1, 1, 0)
    pl.semaphore_wait(barrier, tall_group * wide_group - 1)

    def opposite(step):
        return (-step[0], -step[1])

    def rim_copy(at):
        step = DIRS[at]
        if step[0] == 0:
            source = strip_out.at[0 if step[1] > 0 else 1]
            target = strip_in.at[0 if step[1] > 0 else 1]
        else:
            source_rows = pl.ds(side - HALO if step[0] > 0 else 0, HALO)
            target_rows = pl.ds(0 if step[0] > 0 else side + HALO, HALO)
            if step[1] == 0:
                source = template.at[source_rows]
                target = padded.at[target_rows, pl.ds(LANES, side)]
            else:
                source = template.at[source_rows, pl.ds(last if step[1] > 0 else 0, LANES)]
                target = padded.at[target_rows, pl.ds(0 if step[1] > 0 else side + LANES, LANES)]
        return pltpu.make_async_remote_copy(
            src_ref=source, dst_ref=target, send_sem=rim_send.at[at], recv_sem=rim_recv.at[at],
            device_id=neighbour(step), device_id_type=MESH,
        )

    def label_copy(at):
        return pltpu.make_async_remote_copy(
            src_ref=label, dst_ref=arrived_label.at[at], send_sem=label_send.at[at],
            recv_sem=label_recv.at[at], device_id=neighbour(DIRS[at]), device_id_type=MESH,
        )

    def bucket_copy(at):
        return pltpu.make_async_remote_copy(
            src_ref=outgoing.at[at], dst_ref=arrived.at[at], send_sem=send_sem.at[at],
            recv_sem=recv_sem.at[at], device_id=neighbour(DIRS[at]), device_id_type=MESH,
        )

    def pack_strip(strip, first_col, first_lane):
        lane_group = lax.broadcasted_iota(jnp.int32, (LANES, LANES), 1) // HALO
        packed = jnp.zeros((LANES, LANES), jnp.float32)
        for group in range(side // LANES):
            block = padded[pl.ds(HALO + group * LANES, LANES), pl.ds(first_col, LANES)]
            moved = pltpu.roll(
                block.astype(jnp.float32), (group * HALO - first_lane) % LANES, 1
            )
            packed = jnp.where(lane_group == group, moved, packed)
        strip_out[strip] = packed.astype(jnp.bfloat16)

    loads[0].wait()
    loads[1].wait()
    pack_strip(0, side, LANES - HALO)
    pack_strip(1, LANES, 0)
    for at, step in enumerate(DIRS):
        @pl.when(exists(step))
        def _():
            rim_copy(at).start()
            label_copy(at).start()

    loads[2].wait()
    for at, step in enumerate(DIRS):
        def pack(slot, carry):
            outgoing[at, slot] = held[index[bucket_of(step), slot]]
            return carry

        lax.fori_loop(0, CAP, pack, 0)

        @pl.when(exists(step))
        def _():
            bucket_copy(at).start()

    lane = lax.broadcasted_iota(jnp.int32, (8, side), 1)
    u = ((col * side + lane).astype(jnp.float32) + 0.5) * (2.0 / (side * cols)) - 1.0
    for basis in range(BASES):
        for power_v in range(DEGREE + 1):
            total = jnp.zeros_like(u)
            for power_u in reversed(range(DEGREE + 1 - power_v)):
                total = total * u + coef[basis, term_powers.index((power_u, power_v))]
            inner[basis, power_v] = total

    loads[3].wait()
    wide = padded.shape[1]

    @pl.when(row == 0)
    def _():
        padded[pl.ds(0, HALO)] = jnp.zeros((HALO, wide), jnp.bfloat16)

    @pl.when(row == rows - 1)
    def _():
        padded[pl.ds(side + HALO, HALO)] = jnp.zeros((HALO, wide), jnp.bfloat16)

    @pl.when(col == 0)
    def _():
        padded[:, pl.ds(0, LANES)] = jnp.zeros((padded.shape[0], LANES), jnp.bfloat16)

    @pl.when(col == cols - 1)
    def _():
        padded[:, pl.ds(side + LANES, LANES)] = jnp.zeros((padded.shape[0], LANES), jnp.bfloat16)

    for at, step in enumerate(DIRS):
        @pl.when(exists(opposite(step)))
        def _():
            rim_copy(at).wait_recv()

    def unpack_strip(strip, first_col, first_lane):
        packed = strip_in[strip].astype(jnp.float32)
        for group in range(side // LANES):
            moved = pltpu.roll(packed, (first_lane - group * HALO) % LANES, 1)
            padded[pl.ds(HALO + group * LANES, LANES), pl.ds(first_col, LANES)] = moved.astype(jnp.bfloat16)

    @pl.when(col > 0)
    def _():
        unpack_strip(0, 0, LANES - HALO)

    @pl.when(col < cols - 1)
    def _():
        unpack_strip(1, side + LANES, 0)

    tall = padded.shape[0]
    chunk = tall // 3
    blocks = side // LANES
    for basis in range(BASES):
        across[basis, pl.ds(tall, across.shape[1] - tall)] = jnp.zeros(
            (across.shape[1] - tall, side), jnp.bfloat16
        )

    def row_pass(block, carry):
        first = pl.multiple_of(block * LANES, LANES)
        for part in range(3):
            got = jnp.dot(
                padded[pl.ds(part * chunk, chunk), pl.ds(first, 3 * LANES)],
                band_across[...],
                preferred_element_type=jnp.float32,
            )
            for basis in range(BASES):
                across[basis, pl.ds(part * chunk, chunk), pl.ds(first, LANES)] = got[
                    :, basis * LANES : (basis + 1) * LANES
                ].astype(jnp.bfloat16)
        return carry

    lax.fori_loop(0, blocks, row_pass, 0)

    part_cols = 2 * LANES

    def column_pass(block, carry):
        first = pl.multiple_of(block * LANES, LANES)
        line = lax.broadcasted_iota(jnp.int32, (LANES, part_cols), 0)
        v = ((row * side + first + line).astype(jnp.float32) + 0.5) * (2.0 / (side * rows)) - 1.0
        for part in range(side // part_cols):
            columns = pl.ds(part * part_cols, part_cols)
            total = jnp.zeros((LANES, part_cols), jnp.float32)
            for basis in range(BASES):
                smoothed = jnp.dot(
                    band_down[basis],
                    across[basis, pl.ds(first, 2 * LANES), columns],
                    preferred_element_type=jnp.float32,
                )
                weight = jnp.broadcast_to(inner[basis, DEGREE, 0:1, columns], total.shape)
                for power_v in reversed(range(DEGREE)):
                    weight = weight * v + inner[basis, power_v, 0:1, columns]
                total = total + weight * smoothed
            result[pl.ds(first, LANES), columns] = total
        return carry

    lax.fori_loop(0, blocks, column_pass, 0)
    out = pltpu.make_async_copy(result, matched, out_sem)
    out.start()

    for at, step in enumerate(DIRS):
        @pl.when(exists(step))
        def _():
            rim_copy(at).wait_send()
            label_copy(at).wait_send()
            bucket_copy(at).wait_send()

        @pl.when(exists(opposite(step)))
        def _():
            label_copy(at).wait_recv()
            bucket_copy(at).wait_recv()
    out.wait()


def join_kernel(
    index, label, arrived_label, pieces, arrived, matched, out,
    held, head, following, covered, load_sem,
):
    rows, cols = lax.axis_size("py"), lax.axis_size("px")
    row, col = lax.axis_index("py"), lax.axis_index("px")
    own = pieces.shape[0]
    blocks = head.shape[0]
    per_row = out.shape[1] // LANES

    @pl.when(pl.program_id(0) == 0)
    def _():
        loads = [pltpu.make_async_copy(pieces, held.at[pl.ds(0, own)], load_sem.at[0])]
        for at in range(len(DIRS)):
            loads.append(
                pltpu.make_async_copy(
                    arrived.at[at], held.at[pl.ds(own + at * CAP, CAP)], load_sem.at[at + 1]
                )
            )
        for load in loads:
            load.start()

        def clear(block, carry):
            head[block] = 0
            covered[block] = 0
            return carry

        lax.fori_loop(0, blocks, clear, 0)

        def link(tag, piece):
            @pl.when(tag > 0)
            def _():
                following[piece] = head[tag - 1]
                head[tag - 1] = piece
                covered[tag - 1] = covered[tag - 1] + 1

        def link_own(slot, carry):
            link(label[OWN, slot], index[OWN, slot])
            return carry

        lax.fori_loop(0, CAP, link_own, 0)
        for at, step in enumerate(DIRS):
            r, c = row - step[0], col - step[1]

            @pl.when((r >= 0) & (r < rows) & (c >= 0) & (c < cols))
            def _():
                def link_arrived(slot, carry):
                    link(arrived_label[at, bucket_of(step), slot], own + at * CAP + slot)
                    return carry

                lax.fori_loop(0, CAP, link_arrived, 0)
        for load in loads:
            load.wait()

    for at in range(per_row):
        block = pl.program_id(0) * per_row + at
        count = covered[block]

        def add(_, state):
            piece, total = state
            return following[piece], total + held[piece].astype(jnp.float32)

        _, total = lax.fori_loop(
            0, count, add, (head[block], jnp.zeros((LANES, LANES), jnp.float32))
        )
        share = 1.0 / jnp.full((8, LANES), jnp.maximum(count, 1).astype(jnp.float32))
        columns = pl.ds(at * LANES, LANES)
        out[:, columns] = total * jnp.tile(share, (LANES // 8, 1)) - matched[:, columns]


def on_device(pieces, owner_map, offsets, template, coefficients):
    own, block_side = pieces.shape[0], pieces.shape[1]
    side = template.shape[0]
    blocks = (side // block_side) ** 2
    smem = pl.BlockSpec(memory_space=pltpu.SMEM)
    vmem = pl.BlockSpec(memory_space=pltpu.VMEM)
    anywhere = pl.BlockSpec(memory_space=pl.ANY)
    count = len(DIRS)

    index, label = pl.pallas_call(
        slots_kernel,
        out_shape=[jax.ShapeDtypeStruct((9, LANES), jnp.int32)] * 2,
        in_specs=[smem, smem],
        out_specs=[smem, smem],
        scratch_shapes=[pltpu.SMEM((9,), jnp.int32)],
        name="slots",
    )(owner_map, offsets)

    band_across, band_down = band_tables()
    tall = side + 2 * HALO
    dma = pltpu.SemaphoreType.DMA
    arrived, arrived_label, matched = pl.pallas_call(
        send_kernel,
        out_shape=[
            jax.ShapeDtypeStruct((count, CAP, block_side, block_side), jnp.bfloat16),
            jax.ShapeDtypeStruct((count, 9, LANES), jnp.int32),
            jax.ShapeDtypeStruct((side, side), jnp.float32),
        ],
        in_specs=[smem, smem, anywhere, anywhere, anywhere, vmem, vmem],
        out_specs=[anywhere, anywhere, anywhere],
        scratch_shapes=[
            pltpu.VMEM((own, block_side, block_side), jnp.bfloat16),
            pltpu.VMEM((count, CAP, block_side, block_side), jnp.bfloat16),
            pltpu.VMEM((tall, side + 2 * LANES), jnp.bfloat16),
            pltpu.VMEM((2, LANES, LANES), jnp.bfloat16),
            pltpu.VMEM((2, LANES, LANES), jnp.bfloat16),
            pltpu.VMEM((BASES, side + LANES, side), jnp.bfloat16),
            pltpu.VMEM((BASES, DEGREE + 1, 8, side), jnp.float32),
            pltpu.VMEM((side, side), jnp.float32),
            dma((4,)), dma((count,)), dma((count,)), dma((count,)), dma((count,)),
            dma((count,)), dma((count,)), dma,
        ],
        compiler_params=pltpu.CompilerParams(
            collective_id=0, has_side_effects=True, vmem_limit_bytes=48 << 20
        ),
        name="send",
    )(index, coefficients, label, pieces, template, jnp.asarray(band_across), jnp.asarray(band_down))

    row_block = pl.BlockSpec((block_side, side), lambda i: (i, 0))
    return pl.pallas_call(
        join_kernel,
        grid=(side // block_side,),
        out_shape=jax.ShapeDtypeStruct((side, side), jnp.float32),
        in_specs=[smem, smem, smem, anywhere, anywhere, row_block],
        out_specs=row_block,
        scratch_shapes=[
            pltpu.VMEM((own + count * CAP, block_side, block_side), jnp.bfloat16),
            pltpu.SMEM((blocks,), jnp.int32),
            pltpu.SMEM((own + count * CAP,), jnp.int32),
            pltpu.SMEM((blocks,), jnp.int32),
            dma((count + 1,)),
        ],
        compiler_params=pltpu.CompilerParams(vmem_limit_bytes=32 << 20),
        name="join",
    )(index, label, arrived_label, pieces, arrived, matched)


def solution(mesh):
    in_specs = (P(("py", "px"), None, None), P(("py", "px")), P(("py", "px")), P("py", "px"), P())
    out_specs = P("py", "px")
    return jax.shard_map(
        on_device, mesh=mesh, in_specs=in_specs, out_specs=out_specs, check_vma=False
    )
```

time: 248 us -> 70 us (0.28)
  the two profiles are of different devices: /device:TPU:105 before, /device:TPU:49 now
where the time goes in v1:
time: 70 us; the launch traced here: 69.6 us
  Pallas kernels  58 us (83%)
  local copies, waits for them, and re-layouts  11.5 us (16%)
    pallas_call x1, Pallas kernels, on_device(): pl.pallas_call(send_kernel, out_shape=[jax.ShapeDtypeStruct((count, CAP,...  45.5 us
    unnamed x18, local copies, waits for them, and re-layouts  11.5 us
    pallas_call x1, Pallas kernels, on_device(): pl.pallas_call(join_kernel, grid=(side // block_side,), out_shape=jax.Sha...  9.37 us
    pallas_call x1, Pallas kernels, on_device(): pl.pallas_call(slots_kernel, out_shape=[jax.ShapeDtypeStruct((9, LANES),...  3.13 us

profile of v1, /device:TPU:49, one launch (start us, length us, event | category | flops | bytes accessed | tf_op | source)
XLA Modules:
  0.0 69.6 jit_solution(8529090943698903989)
XLA Ops:
  0.0 3.1 %slots.1 = (s32[9,128]{1,0:T(8,128)}, s32[9,128]{1,0:T(8,128)}) custom-call(s32[64]{0:T(128)} %owner.1, s32[64]{0:T(128)} %offset.1), custom_call_target="tpu_custom_call" | custom-call | tf_op jit(solution)/shard_map/slots/pallas_call | solution.py:375
  3.1 0.0 copy-start
  3.1 1.6 %copy-done = bf16[64,128,128]{2,1,0:T(8,128)(2,1)S(1)} copy-done((bf16[64,128,128]{2,1,0:T(8,128)(2,1)S(1)}, bf16[64,128,128]{2,1,0:T(8,128)(2,1)}, u32[]{:S(2)}) %copy-start) | copy-done | bytes 2097176
  4.7 0.0 copy-start.3
  4.7 1.6 %copy-done.3 = bf16[1024,1024]{1,0:T(8,128)(2,1)S(1)} copy-done((bf16[1024,1024]{1,0:T(8,128)(2,1)S(1)}, bf16[1024,1024]{1,0:T(8,128)(2,1)}, u32[]{:S(2)}) %copy-start.3) | copy-done | bytes 2097176
  6.3 0.0 copy-start.4
  6.3 1.0 %copy-done.4 = bf16[384,384]{1,0:T(8,128)(2,1)S(1)} copy-done((bf16[384,384]{1,0:T(8,128)(2,1)S(1)}, bf16[384,384]{1,0:T(8,128)(2,1)}, u32[]{:S(2)}) %copy-start.4) | copy-done | bytes 294936
  7.3 0.0 copy-start.5
  7.3 0.9 %copy-done.5 = bf16[3,128,256]{2,1,0:T(8,128)(2,1)S(1)} copy-done((bf16[3,128,256]{2,1,0:T(8,128)(2,1)S(1)}, bf16[3,128,256]{2,1,0:T(8,128)(2,1)}, u32[]{:S(2)}) %copy-start.5) | copy-done | bytes 196632
  8.2 0.0 copy-start.6
  8.2 0.7 copy-done.6
  8.9 0.0 copy-start.7
  8.9 0.7 copy-done.7
  9.6 0.0 copy-start.8
  9.6 0.7 copy-done.8
  10.3 45.5 %send.1 = (bf16[8,16,128,128]{3,2,1,0:T(8,128)(2,1)}, s32[8,9,128]{2,1,0:T(8,128)S(1)}, f32[1024,1024]{1,0:T(8,128)}) custom-call(s32[9,128]{1,0:T(8,128)S(1)} %copy-done.6, f32[3,15]{1,0:T(4,128)S(1)} %copy-done.8, s32[9,128]{1,0:T(8,128)S(1)} %copy-done.7, bf16[64,128,128]{2,1,0:T(8,128)(2,1)S(1)} %copy-done, bf16[1024,1024]{1,0:T(8,128)(2,1)S(1)} %copy-done.3, ...), custom_call_target="tpu_custom_call" | custom-call | tf_op jit(solution)/shard_map/send/pallas_call | solution.py:387
  55.8 0.0 copy-start.1
  55.8 2.2 %copy-done.1 = bf16[8,16,128,128]{3,2,1,0:T(8,128)(2,1)S(1)} copy-done((bf16[8,16,128,128]{3,2,1,0:T(8,128)(2,1)S(1)}, bf16[8,16,128,128]{3,2,1,0:T(8,128)(2,1)}, u32[]{:S(2)}) %copy-start.1) | copy-done | bytes 4194328
  58.0 0.0 copy-start.2
  58.0 2.2 %copy-done.2 = f32[1024,1024]{1,0:T(8,128)S(1)} copy-done((f32[1024,1024]{1,0:T(8,128)S(1)}, f32[1024,1024]{1,0:T(8,128)}, u32[]{:S(2)}) %copy-start.2) | copy-done | bytes 4194328
  60.2 9.4 %join.1 = f32[1024,1024]{1,0:T(8,128)} custom-call(s32[9,128]{1,0:T(8,128)S(1)} %copy-done.6, s32[9,128]{1,0:T(8,128)S(1)} %copy-done.7, s32[8,9,128]{2,1,0:T(8,128)S(1)} %get-tuple-element.12.arrived_label, bf16[64,128,128]{2,1,0:T(8,128)(2,1)S(1)} %copy-done, bf16[8,16,128,128]{3,2,1,0:T(8,128)(2,1)S(1)} %copy-done.1, f32[1024,1024]{1,0:T(8,128)S(1)} %copy-done.2), custom_call_target="tpu_custom_call" | custom-call | tf_op jit(solution)/shard_map/join/pallas_call | solution.py:415
Async XLA Ops:
  3.1 1.6 %copy-start = (bf16[64,128,128]{2,1,0:T(8,128)(2,1)S(1)}, bf16[64,128,128]{2,1,0:T(8,128)(2,1)}, u32[]{:S(2)}) copy-start(bf16[64,128,128]{2,1,0:T(8,128)(2,1)} %pieces.3) | copy-start | bytes 6291460
  4.7 1.6 %copy-start.3 = (bf16[1024,1024]{1,0:T(8,128)(2,1)S(1)}, bf16[1024,1024]{1,0:T(8,128)(2,1)}, u32[]{:S(2)}) copy-start(bf16[1024,1024]{1,0:T(8,128)(2,1)} %template.1) | copy-start | bytes 6291460
  6.3 1.0 %copy-start.4 = (bf16[384,384]{1,0:T(8,128)(2,1)S(1)}, bf16[384,384]{1,0:T(8,128)(2,1)}, u32[]{:S(2)}) copy-start(bf16[384,384]{1,0:T(8,128)(2,1)} %constant.4.clone.band_across) | copy-start | bytes 884740
  7.3 0.9 %copy-start.5 = (bf16[3,128,256]{2,1,0:T(8,128)(2,1)S(1)}, bf16[3,128,256]{2,1,0:T(8,128)(2,1)}, u32[]{:S(2)}) copy-start(bf16[3,128,256]{2,1,0:T(8,128)(2,1)} %constant.5.clone.band_down) | copy-start | bytes 589828
  8.2 0.7 %copy-start.6 = (s32[9,128]{1,0:T(8,128)S(1)}, s32[9,128]{1,0:T(8,128)}, u32[]{:S(2)}) copy-start(s32[9,128]{1,0:T(8,128)} %get-tuple-element.10.index) | copy-start | bytes 13828
  8.9 0.7 %copy-start.7 = (s32[9,128]{1,0:T(8,128)S(1)}, s32[9,128]{1,0:T(8,128)}, u32[]{:S(2)}) copy-start(s32[9,128]{1,0:T(8,128)} %get-tuple-element.11.label) | copy-start | bytes 13828
  9.6 0.7 copy-start.8
  55.8 2.2 %copy-start.1 = (bf16[8,16,128,128]{3,2,1,0:T(8,128)(2,1)S(1)}, bf16[8,16,128,128]{3,2,1,0:T(8,128)(2,1)}, u32[]{:S(2)}) copy-start(bf16[8,16,128,128]{3,2,1,0:T(8,128)(2,1)} %get-tuple-element.13.arrived) | copy-start | bytes 12582916
  58.0 2.2 %copy-start.2 = (f32[1024,1024]{1,0:T(8,128)S(1)}, f32[1024,1024]{1,0:T(8,128)}, u32[]{:S(2)}) copy-start(f32[1024,1024]{1,0:T(8,128)} %get-tuple-element.14.matched) | copy-start | bytes 12582916

commit v2 on v1

v2 whole, which is shorter than its diff:
```python
import functools

import jax
import jax.numpy as jnp
import numpy as np
from jax import lax
from jax.experimental import pallas as pl
from jax.experimental.pallas import tpu as pltpu
from jax.sharding import PartitionSpec as P

HALO = 16
CAP = 16
LANES = 128
BASES = 3
DEGREE = 4

sigma_fractions = (0.09375, 0.1875, 0.375)
term_powers = [(degree - power_v, power_v) for degree in range(5) for power_v in range(degree + 1)]

DIRS = ((1, 1), (-1, -1), (1, -1), (-1, 1), (0, 1), (0, -1), (1, 0), (-1, 0))
OWN = 4
MESH = pl.DeviceIdType.MESH


def bucket_of(step):
    return 3 * (step[0] + 1) + step[1] + 1


def gauss_taps():
    positions = np.arange(-HALO, HALO + 1).astype(np.float32)
    stacked = []
    for fraction in sigma_fractions:
        sigma = fraction * HALO
        values = np.exp(-positions * positions / np.float32(2.0 * sigma * sigma))
        stacked.append(values / np.sum(values))
    return np.stack(stacked).astype(jnp.bfloat16)


def band_tables():
    taps = gauss_taps()
    across = np.zeros((3 * LANES, BASES * LANES), taps.dtype)
    down = np.zeros((BASES, LANES, 2 * LANES), taps.dtype)
    for basis in range(BASES):
        for out in range(LANES):
            for tap in range(2 * HALO + 1):
                across[LANES - HALO + out + tap, basis * LANES + out] = taps[basis, tap]
                down[basis, out, out + tap] = taps[basis, tap]
    return across, down


def send_kernel(
    owner, offset, coef, pieces, template, band_across, band_down,
    arrived, tags, matched,
    held, owner_row, offset_row, table, table_scalar, arrived_table,
    outgoing, padded, strip_out, strip_in, across, inner, row_band, down_band,
    load_sem, table_sem, send_sem, recv_sem, label_send, label_recv, rim_send, rim_recv,
):
    rows, cols = lax.axis_size("py"), lax.axis_size("px")
    row, col = lax.axis_index("py"), lax.axis_index("px")
    side = template.shape[0]
    last = side - LANES
    own = held.shape[0]

    def exists(step):
        r, c = row + step[0], col + step[1]
        return (r >= 0) & (r < rows) & (c >= 0) & (c < cols)

    def neighbour(step):
        return (row + step[0], col + step[1])

    body = padded.at[pl.ds(HALO, side)]
    loads = [
        pltpu.make_async_copy(owner, owner_row, load_sem.at[0]),
        pltpu.make_async_copy(offset, offset_row, load_sem.at[1]),
        pltpu.make_async_copy(pieces, held, load_sem.at[2]),
        pltpu.make_async_copy(
            template.at[:, pl.ds(0, LANES)], body.at[:, pl.ds(LANES, LANES)], load_sem.at[3]
        ),
        pltpu.make_async_copy(
            template.at[:, pl.ds(last, LANES)], body.at[:, pl.ds(side, LANES)], load_sem.at[4]
        ),
        pltpu.make_async_copy(
            template.at[:, pl.ds(LANES, side - 2 * LANES)],
            body.at[:, pl.ds(2 * LANES, side - 2 * LANES)],
            load_sem.at[5],
        ),
        pltpu.make_async_copy(band_across, row_band, load_sem.at[6]),
        pltpu.make_async_copy(band_down, down_band, load_sem.at[7]),
    ]
    for load in loads:
        load.start()

    barrier = pltpu.get_barrier_semaphore()
    for step in DIRS:
        @pl.when(exists(step))
        def _():
            pl.semaphore_signal(barrier, inc=1, device_id=neighbour(step), device_id_type=MESH)
    tall_group = 3 - jnp.where(row == 0, 1, 0) - jnp.where(row == rows - 1, 1, 0)
    wide_group = 3 - jnp.where(col == 0, 1, 0) - jnp.where(col == cols - 1, 1, 0)

    loads[0].wait()
    loads[1].wait()
    bucket_id = lax.broadcasted_iota(jnp.int32, (16, own), 0)
    target = jnp.full((16, own), -1, jnp.int32)
    for bucket in range(9):
        tile = (row + bucket // 3 - 1) * cols + col + bucket % 3 - 1
        target = jnp.where(bucket_id == bucket, tile, target)
    belongs = target == jnp.broadcast_to(owner_row[...], (16, own))
    earlier = (
        lax.broadcasted_iota(jnp.int32, (own, own), 0)
        < lax.broadcasted_iota(jnp.int32, (own, own), 1)
    )
    place = jnp.dot(
        jnp.where(belongs, 1.0, 0.0), jnp.where(earlier, 1.0, 0.0),
        preferred_element_type=jnp.float32,
    )
    code = lax.broadcasted_iota(jnp.int32, (16, own), 1) + own * (
        jnp.broadcast_to(offset_row[...], (16, own)) + 1
    )
    code = jnp.where(belongs, code.astype(jnp.float32), 0.0)
    slot_lane = lax.broadcasted_iota(jnp.int32, (16, LANES), 1)
    filled = jnp.zeros((16, LANES), jnp.float32)
    for slot in range(CAP):
        picked = jnp.sum(jnp.where(place == slot, code, 0.0), axis=1, keepdims=True)
        filled = jnp.where(slot_lane == slot, picked, filled)
    table[...] = filled.astype(jnp.int32)
    to_scalar = pltpu.make_async_copy(table, table_scalar, table_sem)
    to_scalar.start()

    loads[2].wait()
    to_scalar.wait()
    pl.semaphore_wait(barrier, tall_group * wide_group - 1)

    def opposite(step):
        return (-step[0], -step[1])

    def rim_copy(at):
        step = DIRS[at]
        if step[0] == 0:
            source = strip_out.at[0 if step[1] > 0 else 1]
            target = strip_in.at[0 if step[1] > 0 else 1]
        else:
            source_rows = pl.ds(side - HALO if step[0] > 0 else 0, HALO)
            target_rows = pl.ds(0 if step[0] > 0 else side + HALO, HALO)
            if step[1] == 0:
                source = template.at[source_rows]
                target = padded.at[target_rows, pl.ds(LANES, side)]
            else:
                source = template.at[source_rows, pl.ds(last if step[1] > 0 else 0, LANES)]
                target = padded.at[target_rows, pl.ds(0 if step[1] > 0 else side + LANES, LANES)]
        return pltpu.make_async_remote_copy(
            src_ref=source, dst_ref=target, send_sem=rim_send.at[at], recv_sem=rim_recv.at[at],
            device_id=neighbour(step), device_id_type=MESH,
        )

    def label_copy(at):
        return pltpu.make_async_remote_copy(
            src_ref=table, dst_ref=arrived_table.at[at], send_sem=label_send.at[at],
            recv_sem=label_recv.at[at], device_id=neighbour(DIRS[at]), device_id_type=MESH,
        )

    def bucket_copy(at, slots=pl.ds(0, CAP)):
        return pltpu.make_async_remote_copy(
            src_ref=outgoing.at[at, slots], dst_ref=arrived.at[at, slots], send_sem=send_sem.at[at],
            recv_sem=recv_sem.at[at], device_id=neighbour(DIRS[at]), device_id_type=MESH,
        )

    def pack_strip(strip, first_col, first_lane):
        lane_group = lax.broadcasted_iota(jnp.int32, (LANES, LANES), 1) // HALO
        packed = jnp.zeros((LANES, LANES), jnp.float32)
        for group in range(side // LANES):
            block = padded[pl.ds(HALO + group * LANES, LANES), pl.ds(first_col, LANES)]
            moved = pltpu.roll(
                block.astype(jnp.float32), (group * HALO - first_lane) % LANES, 1
            )
            packed = jnp.where(lane_group == group, moved, packed)
        strip_out[strip] = packed.astype(jnp.bfloat16)

    def send_slot(slot, carry):
        for at, step in enumerate(DIRS):
            piece = table_scalar[bucket_of(step), slot] & (own - 1)
            outgoing[at, slot] = held[piece]

            @pl.when(exists(step))
            def _():
                bucket_copy(at, pl.ds(slot, 1)).start()
        arrived[len(DIRS), slot] = held[table_scalar[OWN, slot] & (own - 1)]
        return carry

    lax.fori_loop(0, 2, send_slot, 0)
    loads[3].wait()
    loads[4].wait()
    pack_strip(0, side, LANES - HALO)
    pack_strip(1, LANES, 0)
    for at, step in enumerate(DIRS):
        @pl.when(exists(step))
        def _():
            rim_copy(at).start()
            label_copy(at).start()
    lax.fori_loop(2, CAP, send_slot, 0)

    lane = lax.broadcasted_iota(jnp.int32, (8, side), 1)
    u = ((col * side + lane).astype(jnp.float32) + 0.5) * (2.0 / (side * cols)) - 1.0
    for basis in range(BASES):
        for power_v in range(DEGREE + 1):
            total = jnp.zeros_like(u)
            for power_u in reversed(range(DEGREE + 1 - power_v)):
                total = total * u + coef[basis, term_powers.index((power_u, power_v))]
            inner[basis, power_v] = total

    for load in loads[5:]:
        load.wait()
    wide = padded.shape[1]

    @pl.when(row == 0)
    def _():
        padded[pl.ds(0, HALO)] = jnp.zeros((HALO, wide), jnp.bfloat16)

    @pl.when(row == rows - 1)
    def _():
        padded[pl.ds(side + HALO, HALO)] = jnp.zeros((HALO, wide), jnp.bfloat16)

    @pl.when(col == 0)
    def _():
        padded[:, pl.ds(0, LANES)] = jnp.zeros((padded.shape[0], LANES), jnp.bfloat16)

    @pl.when(col == cols - 1)
    def _():
        padded[:, pl.ds(side + LANES, LANES)] = jnp.zeros((padded.shape[0], LANES), jnp.bfloat16)

    for at, step in enumerate(DIRS):
        @pl.when(exists(opposite(step)))
        def _():
            rim_copy(at).wait_recv()

    def unpack_strip(strip, first_col, first_lane):
        packed = strip_in[strip].astype(jnp.float32)
        for group in range(side // LANES):
            moved = pltpu.roll(packed, (first_lane - group * HALO) % LANES, 1)
            padded[pl.ds(HALO + group * LANES, LANES), pl.ds(first_col, LANES)] = moved.astype(jnp.bfloat16)

    @pl.when(col > 0)
    def _():
        unpack_strip(0, 0, LANES - HALO)

    @pl.when(col < cols - 1)
    def _():
        unpack_strip(1, side + LANES, 0)

    tall = padded.shape[0]
    chunk = tall // 3
    blocks = side // LANES
    for basis in range(BASES):
        across[basis, pl.ds(tall, across.shape[1] - tall)] = jnp.zeros(
            (across.shape[1] - tall, side), jnp.bfloat16
        )

    def row_pass(block, carry):
        first = pl.multiple_of(block * LANES, LANES)
        for part in range(3):
            got = jnp.dot(
                padded[pl.ds(part * chunk, chunk), pl.ds(first, 3 * LANES)],
                row_band[...],
                preferred_element_type=jnp.float32,
            )
            for basis in range(BASES):
                across[basis, pl.ds(part * chunk, chunk), pl.ds(first, LANES)] = got[
                    :, basis * LANES : (basis + 1) * LANES
                ].astype(jnp.bfloat16)
        return carry

    lax.fori_loop(0, blocks, row_pass, 0)

    part_cols = 2 * LANES

    def column_pass(block, carry):
        first = pl.multiple_of(block * LANES, LANES)
        line = lax.broadcasted_iota(jnp.int32, (LANES, part_cols), 0)
        v = ((row * side + first + line).astype(jnp.float32) + 0.5) * (2.0 / (side * rows)) - 1.0
        for part in range(side // part_cols):
            columns = pl.ds(part * part_cols, part_cols)
            total = jnp.zeros((LANES, part_cols), jnp.float32)
            for basis in range(BASES):
                smoothed = jnp.dot(
                    down_band[basis],
                    across[basis, pl.ds(first, 2 * LANES), columns],
                    preferred_element_type=jnp.float32,
                )
                weight = jnp.broadcast_to(inner[basis, DEGREE, 0:1, columns], total.shape)
                for power_v in reversed(range(DEGREE)):
                    weight = weight * v + inner[basis, power_v, 0:1, columns]
                total = total + weight * smoothed
            matched[pl.ds(first, LANES), columns] = total
        return carry

    lax.fori_loop(0, blocks, column_pass, 0)

    for at, step in enumerate(DIRS):
        tags[pl.ds(at, 1)] = jnp.zeros((1, LANES), jnp.int32)

        @pl.when(exists(opposite(step)))
        def _():
            label_copy(at).wait_recv()
            tags[pl.ds(at, 1)] = arrived_table[at, pl.ds(bucket_of(step), 1)]
    tags[pl.ds(len(DIRS), 1)] = table[pl.ds(OWN, 1)]

    for at, step in enumerate(DIRS):
        @pl.when(exists(step))
        def _():
            rim_copy(at).wait_send()
            label_copy(at).wait_send()
            bucket_copy(at).wait_send()

        @pl.when(exists(opposite(step)))
        def _():
            bucket_copy(at).wait_recv()


def join_kernel(own, tags, arrived, matched, out, result, head, following, covered, out_sem):
    blocks = head.shape[0]
    side = out.shape[1]
    per_row = side // LANES

    def clear(block, carry):
        head[block] = 0
        covered[block] = 0
        return carry

    lax.fori_loop(0, blocks, clear, 0, unroll=8)

    def link(code, piece):
        tag = lax.div(code, own)

        @pl.when(tag > 0)
        def _():
            following[piece] = head[tag - 1]
            head[tag - 1] = piece
            covered[tag - 1] = covered[tag - 1] + 1

    def link_slot(slot, carry):
        for at in range(len(DIRS) + 1):
            link(tags[at, slot], at * CAP + slot)
        return carry

    lax.fori_loop(0, CAP, link_slot, 0)

    def out_copy(block_row):
        lines = pl.ds(pl.multiple_of(block_row * LANES, LANES), LANES)
        return pltpu.make_async_copy(result.at[lines], out.at[lines], out_sem.at[block_row])

    def join_row(block_row, carry):
        lines = pl.ds(pl.multiple_of(block_row * LANES, LANES), LANES)
        for at in range(per_row):
            block = block_row * per_row + at
            count = covered[block]

            def add(_, state):
                piece, total = state
                return following[piece], total + arrived[lax.div(piece, CAP), piece & (CAP - 1)].astype(jnp.float32)

            _, total = lax.fori_loop(
                0, count, add, (head[block], jnp.zeros((LANES, LANES), jnp.float32))
            )
            share = 1.0 / jnp.full((8, LANES), jnp.maximum(count, 1).astype(jnp.float32))
            columns = pl.ds(at * LANES, LANES)
            result[lines, columns] = total * jnp.tile(share, (LANES // 8, 1)) - matched[lines, columns]
        out_copy(block_row).start()
        return carry

    lax.fori_loop(0, per_row, join_row, 0)
    for block_row in range(per_row):
        out_copy(block_row).wait()


def on_device(pieces, owner_map, offsets, template, coefficients):
    own, block_side = pieces.shape[0], pieces.shape[1]
    side = template.shape[0]
    blocks = (side // block_side) ** 2
    smem = pl.BlockSpec(memory_space=pltpu.SMEM)
    vmem = pl.BlockSpec(memory_space=pltpu.VMEM)
    hbm = pl.BlockSpec(memory_space=pltpu.HBM)
    count = len(DIRS)

    band_across, band_down = band_tables()
    tall = side + 2 * HALO
    dma = pltpu.SemaphoreType.DMA
    arrived, tags, matched = pl.pallas_call(
        send_kernel,
        out_shape=[
            jax.ShapeDtypeStruct((count + 1, CAP, block_side, block_side), jnp.bfloat16),
            jax.ShapeDtypeStruct((16, LANES), jnp.int32),
            jax.ShapeDtypeStruct((side, side), jnp.float32),
        ],
        in_specs=[hbm, hbm, smem, hbm, hbm, hbm, hbm],
        out_specs=[vmem, vmem, vmem],
        scratch_shapes=[
            pltpu.VMEM((own, block_side, block_side), jnp.bfloat16),
            pltpu.VMEM((1, own), jnp.int32),
            pltpu.VMEM((1, own), jnp.int32),
            pltpu.VMEM((16, LANES), jnp.int32),
            pltpu.SMEM((16, LANES), jnp.int32),
            pltpu.VMEM((count, 16, LANES), jnp.int32),
            pltpu.VMEM((count, CAP, block_side, block_side), jnp.bfloat16),
            pltpu.VMEM((tall, side + 2 * LANES), jnp.bfloat16),
            pltpu.VMEM((2, LANES, LANES), jnp.bfloat16),
            pltpu.VMEM((2, LANES, LANES), jnp.bfloat16),
            pltpu.VMEM((BASES, side + LANES, side), jnp.bfloat16),
            pltpu.VMEM((BASES, DEGREE + 1, 8, side), jnp.float32),
            pltpu.VMEM(band_across.shape, jnp.bfloat16),
            pltpu.VMEM(band_down.shape, jnp.bfloat16),
            dma((8,)), dma, dma((count,)), dma((count,)), dma((count,)), dma((count,)),
            dma((count,)), dma((count,)),
        ],
        compiler_params=pltpu.CompilerParams(
            collective_id=0, has_side_effects=True, vmem_limit_bytes=40 << 20
        ),
        name="send",
    )(
        *(
            pltpu.with_memory_space_constraint(array, pltpu.HBM)
            for array in (
                owner_map.reshape(1, own), offsets.reshape(1, own), coefficients, pieces,
                template, jnp.asarray(band_across), jnp.asarray(band_down),
            )
        )
    )
    return pl.pallas_call(
        functools.partial(join_kernel, own),
        out_shape=jax.ShapeDtypeStruct((side, side), jnp.float32),
        in_specs=[smem, vmem, vmem],
        out_specs=hbm,
        scratch_shapes=[
            pltpu.VMEM((side, side), jnp.float32),
            pltpu.SMEM((blocks,), jnp.int32),
            pltpu.SMEM(((count + 1) * CAP,), jnp.int32),
            pltpu.SMEM((blocks,), jnp.int32),
            dma((side // block_side,)),
        ],
        compiler_params=pltpu.CompilerParams(vmem_limit_bytes=32 << 20),
        name="join",
    )(tags, arrived, matched)


def solution(mesh):
    in_specs = (P(("py", "px"), None, None), P(("py", "px")), P(("py", "px")), P("py", "px"), P())
    out_specs = P("py", "px")
    return jax.shard_map(
        on_device, mesh=mesh, in_specs=in_specs, out_specs=out_specs, check_vma=False
    )
```

time: 70 us -> 47.6 us (0.68)
  the two profiles are of different devices: /device:TPU:49 before, /device:TPU:105 now
where the time goes in v2:
time: 47.6 us; the launch traced here: 47.5 us
  Pallas kernels  47.5 us (100%)
    pallas_call x1, Pallas kernels, on_device(): pl.pallas_call(send_kernel, out_shape=[jax.ShapeDtypeStruct((count + 1, C...  42.6 us
    pallas_call x1, Pallas kernels, on_device(): pl.pallas_call(functools.partial(join_kernel, own), out_shape=jax.ShapeDt...  4.87 us

profile of v2, /device:TPU:105, one launch (start us, length us, event | category | flops | bytes accessed | tf_op | source)
XLA Modules:
  0.0 47.5 jit_solution(12348083263384867279)
XLA Ops:
  0.0 42.6 %send.1 = (bf16[9,16,128,128]{3,2,1,0:T(8,128)(2,1)S(1)}, s32[16,128]{1,0:T(8,128)S(1)}, f32[1024,1024]{1,0:T(8,128)S(1)}) custom-call(s32[1,64]{1,0:T(1,128)} %bitcast.2, s32[1,64]{1,0:T(1,128)} %bitcast.3, f32[3,15]{1,0:T(4,128)} %coef.1, bf16[64,128,128]{2,1,0:T(8,128)(2,1)} %pieces.1, bf16[1024,1024]{1,0:T(8,128)(2,1)} %template.1, ...), custom_call_target="tpu_custom_call" | custom-call | tf_op jit(solution)/shard_map/send/pallas_call | solution.py:387
  42.6 4.9 %join.1 = f32[1024,1024]{1,0:T(8,128)} custom-call(s32[16,128]{1,0:T(8,128)S(1)} %get-tuple-element.8.tags, bf16[9,16,128,128]{3,2,1,0:T(8,128)(2,1)S(1)} %get-tuple-element.9.arrived, f32[1024,1024]{1,0:T(8,128)S(1)} %get-tuple-element.10.matched), custom_call_target="tpu_custom_call" | custom-call | tf_op jit(solution)/shard_map/join/pallas_call | solution.py:427

commit v3 on v2

--- a/solution.py
+++ b/solution.py
@@ -48,11 +48,68 @@
     return across, down
 
 
+def sort_plan(own, per_row, tags, plan, share):
+    count = len(DIRS)
+    blocks = per_row * per_row
+    shape = (blocks, LANES)
+    code = tags[...]
+    block_tag = lax.shift_right_logical(code, own.bit_length() - 1).astype(jnp.float32)
+    spread = jnp.zeros((8, LANES), jnp.float32)
+    for at in range(count):
+        one = jnp.broadcast_to(block_tag[at : at + 1], (8, LANES))
+        spread = spread + pltpu.roll(one, at * CAP, 1)
+    groups = (spread[0:1], block_tag[count : count + 1])
+
+    block_id = lax.broadcasted_iota(jnp.int32, shape, 0).astype(jnp.float32)
+    before = jnp.where(
+        lax.broadcasted_iota(jnp.int32, (LANES, LANES), 0)
+        < lax.broadcasted_iota(jnp.int32, (LANES, LANES), 1), 1.0, 0.0,
+    )
+    lower = jnp.where(
+        lax.broadcasted_iota(jnp.int32, (blocks, blocks), 1)
+        < lax.broadcasted_iota(jnp.int32, (blocks, blocks), 0), 1.0, 0.0,
+    )
+    hits = [jnp.where(jnp.broadcast_to(tag, shape) == block_id + 1, 1.0, 0.0) for tag in groups]
+    sums = [jnp.broadcast_to(jnp.sum(hit, axis=1, keepdims=True), shape) for hit in hits]
+    covered = sums[0] + sums[1]
+    first = jnp.dot(lower, covered, preferred_element_type=jnp.float32)
+    ahead = (first, first + sums[0])
+
+    line = lax.broadcasted_iota(jnp.int32, (8, LANES), 0)
+    lane = lax.broadcasted_iota(jnp.int32, (8, LANES), 1).astype(jnp.float32)
+    target = lax.broadcasted_iota(jnp.int32, (2 * LANES, LANES), 0).astype(jnp.float32)
+    over_lanes = (((1,), (1,)), ((), ()))
+    listed = jnp.zeros((8, 2 * LANES), jnp.float32)
+    ends = jnp.zeros((8, 2 * LANES), jnp.float32)
+    for group in range(2):
+        hit, tag = hits[group], groups[group]
+        rank = ahead[group] + jnp.dot(hit, before, preferred_element_type=jnp.float32)
+        place = jnp.sum(hit * rank, axis=0, keepdims=True)
+        shares = jnp.sum(hit * covered, axis=0, keepdims=True)
+        place = jnp.where(tag > 0, place, -1.0)
+        chosen = jnp.where(jnp.broadcast_to(place, target.shape) == target, 1.0, 0.0)
+        values = jnp.where(line == 0, lane + group * LANES, 0.0)
+        values = jnp.where(line == 1, jnp.broadcast_to(tag - 1, values.shape), values)
+        values = jnp.where(line == 2, jnp.broadcast_to(shares, values.shape), values)
+        listed = listed + lax.dot_general(
+            values, chosen, over_lanes, preferred_element_type=jnp.float32
+        )
+        wide_tag = jnp.broadcast_to(tag, target.shape)
+        inside = jnp.where((wide_tag > 0) & (wide_tag <= (target + 1) * per_row), 1.0, 0.0)
+        ends = ends + lax.dot_general(
+            jnp.ones((8, LANES), jnp.float32), inside, over_lanes,
+            preferred_element_type=jnp.float32,
+        )
+    wide_line = lax.broadcasted_iota(jnp.int32, listed.shape, 0)
+    plan[...] = jnp.where(wide_line == 2, ends, listed).astype(jnp.int32)
+    share[...] = 1.0 / jnp.maximum(listed, 1.0)
+
+
 def send_kernel(
     owner, offset, coef, pieces, template, band_across, band_down,
-    arrived, tags, matched,
+    arrived, plan, share, matched,
     held, owner_row, offset_row, table, table_scalar, arrived_table,
-    outgoing, padded, strip_out, strip_in, across, inner, row_band, down_band,
+    tags, outgoing, padded, strip_out, strip_in, across, inner, row_band, down_band,
     load_sem, table_sem, send_sem, recv_sem, label_send, label_recv, rim_send, rim_recv,
 ):
     rows, cols = lax.axis_size("py"), lax.axis_size("px")
@@ -68,17 +125,23 @@
     def neighbour(step):
         return (row + step[0], col + step[1])
 
+    barrier = pltpu.get_barrier_semaphore()
+    for step in DIRS:
+        @pl.when(exists(step))
+        def _():
+            pl.semaphore_signal(barrier, inc=1, device_id=neighbour(step), device_id_type=MESH)
+
     body = padded.at[pl.ds(HALO, side)]
     loads = [
         pltpu.make_async_copy(owner, owner_row, load_sem.at[0]),
         pltpu.make_async_copy(offset, offset_row, load_sem.at[1]),
-        pltpu.make_async_copy(pieces, held, load_sem.at[2]),
         pltpu.make_async_copy(
-            template.at[:, pl.ds(0, LANES)], body.at[:, pl.ds(LANES, LANES)], load_sem.at[3]
+            template.at[:, pl.ds(0, LANES)], body.at[:, pl.ds(LANES, LANES)], load_sem.at[2]
         ),
         pltpu.make_async_copy(
-            template.at[:, pl.ds(last, LANES)], body.at[:, pl.ds(side, LANES)], load_sem.at[4]
+            template.at[:, pl.ds(last, LANES)], body.at[:, pl.ds(side, LANES)], load_sem.at[3]
         ),
+        pltpu.make_async_copy(pieces, held, load_sem.at[4]),
         pltpu.make_async_copy(
             template.at[:, pl.ds(LANES, side - 2 * LANES)],
             body.at[:, pl.ds(2 * LANES, side - 2 * LANES)],
@@ -89,14 +152,6 @@
     ]
     for load in loads:
         load.start()
-
-    barrier = pltpu.get_barrier_semaphore()
-    for step in DIRS:
-        @pl.when(exists(step))
-        def _():
-            pl.semaphore_signal(barrier, inc=1, device_id=neighbour(step), device_id_type=MESH)
-    tall_group = 3 - jnp.where(row == 0, 1, 0) - jnp.where(row == rows - 1, 1, 0)
-    wide_group = 3 - jnp.where(col == 0, 1, 0) - jnp.where(col == cols - 1, 1, 0)
 
     loads[0].wait()
     loads[1].wait()
@@ -126,10 +181,6 @@
     table[...] = filled.astype(jnp.int32)
     to_scalar = pltpu.make_async_copy(table, table_scalar, table_sem)
     to_scalar.start()
-
-    loads[2].wait()
-    to_scalar.wait()
-    pl.semaphore_wait(barrier, tall_group * wide_group - 1)
 
     def opposite(step):
         return (-step[0], -step[1])
@@ -187,17 +238,21 @@
         arrived[len(DIRS), slot] = held[table_scalar[OWN, slot] & (own - 1)]
         return carry
 
-    lax.fori_loop(0, 2, send_slot, 0)
+    loads[2].wait()
     loads[3].wait()
-    loads[4].wait()
     pack_strip(0, side, LANES - HALO)
     pack_strip(1, LANES, 0)
+    tall_group = 3 - jnp.where(row == 0, 1, 0) - jnp.where(row == rows - 1, 1, 0)
+    wide_group = 3 - jnp.where(col == 0, 1, 0) - jnp.where(col == cols - 1, 1, 0)
+    pl.semaphore_wait(barrier, tall_group * wide_group - 1)
     for at, step in enumerate(DIRS):
         @pl.when(exists(step))
         def _():
             rim_copy(at).start()
             label_copy(at).start()
-    lax.fori_loop(2, CAP, send_slot, 0)
+    loads[4].wait()
+    to_scalar.wait()
+    lax.fori_loop(0, CAP, send_slot, 0)
 
     lane = lax.broadcasted_iota(jnp.int32, (8, side), 1)
     u = ((col * side + lane).astype(jnp.float32) + 0.5) * (2.0 / (side * cols)) - 1.0
@@ -289,7 +344,7 @@
                 weight = jnp.broadcast_to(inner[basis, DEGREE, 0:1, columns], total.shape)
                 for power_v in reversed(range(DEGREE)):
                     weight = weight * v + inner[basis, power_v, 0:1, columns]
-                total = total + weight * smoothed
+                total = total - weight * smoothed
             matched[pl.ds(first, LANES), columns] = total
         return carry
 
@@ -303,6 +358,7 @@
             label_copy(at).wait_recv()
             tags[pl.ds(at, 1)] = arrived_table[at, pl.ds(bucket_of(step), 1)]
     tags[pl.ds(len(DIRS), 1)] = table[pl.ds(OWN, 1)]
+    sort_plan(own, side // LANES, tags, plan, share)
 
     for at, step in enumerate(DIRS):
         @pl.when(exists(step))
@@ -316,56 +372,32 @@
             bucket_copy(at).wait_recv()
 
 
-def join_kernel(own, tags, arrived, matched, out, result, head, following, covered, out_sem):
-    blocks = head.shape[0]
+def join_kernel(plan, share, arrived, matched, out, total, out_sem):
     side = out.shape[1]
     per_row = side // LANES
 
-    def clear(block, carry):
-        head[block] = 0
-        covered[block] = 0
-        return carry
-
-    lax.fori_loop(0, blocks, clear, 0, unroll=8)
-
-    def link(code, piece):
-        tag = lax.div(code, own)
-
-        @pl.when(tag > 0)
-        def _():
-            following[piece] = head[tag - 1]
-            head[tag - 1] = piece
-            covered[tag - 1] = covered[tag - 1] + 1
-
-    def link_slot(slot, carry):
-        for at in range(len(DIRS) + 1):
-            link(tags[at, slot], at * CAP + slot)
-        return carry
-
-    lax.fori_loop(0, CAP, link_slot, 0)
+    def row_lines(block_row):
+        return pl.ds(pl.multiple_of(block_row * LANES, LANES), LANES)
 
     def out_copy(block_row):
-        lines = pl.ds(pl.multiple_of(block_row * LANES, LANES), LANES)
-        return pltpu.make_async_copy(result.at[lines], out.at[lines], out_sem.at[block_row])
-
-    def join_row(block_row, carry):
-        lines = pl.ds(pl.multiple_of(block_row * LANES, LANES), LANES)
-        for at in range(per_row):
-            block = block_row * per_row + at
-            count = covered[block]
-
-            def add(_, state):
-                piece, total = state
-                return following[piece], total + arrived[lax.div(piece, CAP), piece & (CAP - 1)].astype(jnp.float32)
-
-            _, total = lax.fori_loop(
-                0, count, add, (head[block], jnp.zeros((LANES, LANES), jnp.float32))
-            )
-            share = 1.0 / jnp.full((8, LANES), jnp.maximum(count, 1).astype(jnp.float32))
-            columns = pl.ds(at * LANES, LANES)
-            result[lines, columns] = total * jnp.tile(share, (LANES // 8, 1)) - matched[lines, columns]
+        lines = row_lines(block_row)
+        return pltpu.make_async_copy(total.at[lines], out.at[lines], out_sem.at[block_row])
+
+    def join_row(block_row, start):
+        end = plan[2, block_row]
+        lines = row_lines(block_row)
+
+        def add(at, carry):
+            slot = plan[0, at]
+            column = pl.multiple_of((plan[1, at] - block_row * per_row) * LANES, LANES)
+            columns = pl.ds(column, LANES)
+            piece = arrived[lax.div(slot, CAP), slot & (CAP - 1)].astype(jnp.float32)
+            total[lines, columns] = total[lines, columns] + share[2, at] * piece
+            return carry
+
+        lax.fori_loop(start, end, add, 0)
         out_copy(block_row).start()
-        return carry
+        return end
 
     lax.fori_loop(0, per_row, join_row, 0)
     for block_row in range(per_row):
@@ -375,7 +407,6 @@
 def on_device(pieces, owner_map, offsets, template, coefficients):
     own, block_side = pieces.shape[0], pieces.shape[1]
     side = template.shape[0]
-    blocks = (side // block_side) ** 2
     smem = pl.BlockSpec(memory_space=pltpu.SMEM)
     vmem = pl.BlockSpec(memory_space=pltpu.VMEM)
     hbm = pl.BlockSpec(memory_space=pltpu.HBM)
@@ -384,15 +415,16 @@
     band_across, band_down = band_tables()
     tall = side + 2 * HALO
     dma = pltpu.SemaphoreType.DMA
-    arrived, tags, matched = pl.pallas_call(
+    arrived, plan, share, matched = pl.pallas_call(
         send_kernel,
         out_shape=[
             jax.ShapeDtypeStruct((count + 1, CAP, block_side, block_side), jnp.bfloat16),
-            jax.ShapeDtypeStruct((16, LANES), jnp.int32),
+            jax.ShapeDtypeStruct((8, 2 * LANES), jnp.int32),
+            jax.ShapeDtypeStruct((8, 2 * LANES), jnp.float32),
             jax.ShapeDtypeStruct((side, side), jnp.float32),
         ],
         in_specs=[hbm, hbm, smem, hbm, hbm, hbm, hbm],
-        out_specs=[vmem, vmem, vmem],
+        out_specs=[vmem, vmem, vmem, vmem],
         scratch_shapes=[
             pltpu.VMEM((own, block_side, block_side), jnp.bfloat16),
             pltpu.VMEM((1, own), jnp.int32),
@@ -400,6 +432,7 @@
             pltpu.VMEM((16, LANES), jnp.int32),
             pltpu.SMEM((16, LANES), jnp.int32),
             pltpu.VMEM((count, 16, LANES), jnp.int32),
+            pltpu.VMEM((16, LANES), jnp.int32),
             pltpu.VMEM((count, CAP, block_side, block_side), jnp.bfloat16),
             pltpu.VMEM((tall, side + 2 * LANES), jnp.bfloat16),
             pltpu.VMEM((2, LANES, LANES), jnp.bfloat16),
@@ -424,21 +457,17 @@
             )
         )
     )
-    return pl.pallas_call(
-        functools.partial(join_kernel, own),
-        out_shape=jax.ShapeDtypeStruct((side, side), jnp.float32),
-        in_specs=[smem, vmem, vmem],
-        out_specs=hbm,
-        scratch_shapes=[
-            pltpu.VMEM((side, side), jnp.float32),
-            pltpu.SMEM((blocks,), jnp.int32),
-            pltpu.SMEM(((count + 1) * CAP,), jnp.int32),
-            pltpu.SMEM((blocks,), jnp.int32),
-            dma((side // block_side,)),
-        ],
+    joined, _ = pl.pallas_call(
+        join_kernel,
+        out_shape=[jax.ShapeDtypeStruct((side, side), jnp.float32)] * 2,
+        in_specs=[smem, smem, vmem, vmem],
+        out_specs=[hbm, vmem],
+        input_output_aliases={3: 1},
+        scratch_shapes=[dma((side // block_side,))],
         compiler_params=pltpu.CompilerParams(vmem_limit_bytes=32 << 20),
         name="join",
-    )(tags, arrived, matched)
+    )(plan, share, arrived, matched)
+    return joined
 
 
 def solution(mesh):

time: 47.6 us -> 46.1 us (0.968)
  Pallas kernels: 47.5 us -> 45.8 us
    pallas_call x1, Pallas kernels: 4.87 us -> 3.04 us  [on_device(): pl.pallas_call(join_kernel, out_shape=[jax.ShapeDtypeStruct((side, side),...]
where the time goes in v3:
time: 46.1 us; the launch traced here: 45.8 us
  Pallas kernels  45.8 us (99%)
    pallas_call x1, Pallas kernels, on_device(): pl.pallas_call(send_kernel, out_shape=[jax.ShapeDtypeStruct((count + 1, C...  42.8 us
    pallas_call x1, Pallas kernels, on_device(): pl.pallas_call(join_kernel, out_shape=[jax.ShapeDtypeStruct((side, side),...  3.04 us

profile of v3, /device:TPU:105, one launch (start us, length us, event | category | flops | bytes accessed | tf_op | source)
XLA Modules:
  0.0 45.8 jit_solution(6759033455345279075)
XLA Ops:
  0.0 42.8 %send.1 = (bf16[9,16,128,128]{3,2,1,0:T(8,128)(2,1)S(1)}, s32[8,256]{1,0:T(8,128)S(1)}, f32[8,256]{1,0:T(8,128)S(1)}, f32[1024,1024]{1,0:T(8,128)S(1)}) custom-call(s32[1,64]{1,0:T(1,128)} %bitcast.2, s32[1,64]{1,0:T(1,128)} %bitcast.3, f32[3,15]{1,0:T(4,128)} %coef.1, bf16[64,128,128]{2,1,0:T(8,128)(2,1)} %pieces.1, bf16[1024,1024]{1,0:T(8,128)(2,1)} %template.1, ...), custom_call_target="tpu_custom_call" | custom-call | tf_op jit(solution)/shard_map/send/pallas_call | solution.py:418
  42.8 3.0 %join.1 = (f32[1024,1024]{1,0:T(8,128)}, f32[1024,1024]{1,0:T(8,128)S(1)}) custom-call(s32[8,256]{1,0:T(8,128)S(1)} %get-tuple-element.10.plan, f32[8,256]{1,0:T(8,128)S(1)} %get-tuple-element.11.share, bf16[9,16,128,128]{3,2,1,0:T(8,128)(2,1)S(1)} %get-tuple-element.12.arrived, ...), custom_call_target="tpu_custom_call", output_to_operand_aliasing={{1}: (3, {})} | custom-call | tf_op jit(solution)/shard_map/join/pallas_call | solution.py:460

commit v4 on v3

--- a/solution.py
+++ b/solution.py
@@ -48,7 +48,7 @@
     return across, down
 
 
-def sort_plan(own, per_row, tags, plan, share):
+def sort_plan(own, per_row, tags, plan):
     count = len(DIRS)
     blocks = per_row * per_row
     shape = (blocks, LANES)
@@ -101,14 +101,13 @@
             preferred_element_type=jnp.float32,
         )
     wide_line = lax.broadcasted_iota(jnp.int32, listed.shape, 0)
-    plan[...] = jnp.where(wide_line == 2, ends, listed).astype(jnp.int32)
-    share[...] = 1.0 / jnp.maximum(listed, 1.0)
+    plan[...] = jnp.where(wide_line == 3, ends, listed).astype(jnp.int32)
 
 
 def send_kernel(
-    owner, offset, coef, pieces, template, band_across, band_down,
-    arrived, plan, share, matched,
-    held, owner_row, offset_row, table, table_scalar, arrived_table,
+    owner, offset, coef_hbm, pieces, template, band_across, band_down,
+    arrived, plan, matched,
+    held, coef, owner_row, offset_row, table, rows_out, table_scalar, arrived_table,
     tags, outgoing, padded, strip_out, strip_in, across, inner, row_band, down_band,
     load_sem, table_sem, send_sem, recv_sem, label_send, label_recv, rim_send, rim_recv,
 ):
@@ -133,14 +132,14 @@
 
     body = padded.at[pl.ds(HALO, side)]
     loads = [
-        pltpu.make_async_copy(owner, owner_row, load_sem.at[0]),
-        pltpu.make_async_copy(offset, offset_row, load_sem.at[1]),
         pltpu.make_async_copy(
-            template.at[:, pl.ds(0, LANES)], body.at[:, pl.ds(LANES, LANES)], load_sem.at[2]
+            template.at[:, pl.ds(0, LANES)], body.at[:, pl.ds(LANES, LANES)], load_sem.at[0]
         ),
         pltpu.make_async_copy(
-            template.at[:, pl.ds(last, LANES)], body.at[:, pl.ds(side, LANES)], load_sem.at[3]
+            template.at[:, pl.ds(last, LANES)], body.at[:, pl.ds(side, LANES)], load_sem.at[1]
         ),
+        pltpu.make_async_copy(owner, owner_row, load_sem.at[2]),
+        pltpu.make_async_copy(offset, offset_row, load_sem.at[3]),
         pltpu.make_async_copy(pieces, held, load_sem.at[4]),
         pltpu.make_async_copy(
             template.at[:, pl.ds(LANES, side - 2 * LANES)],
@@ -149,38 +148,10 @@
         ),
         pltpu.make_async_copy(band_across, row_band, load_sem.at[6]),
         pltpu.make_async_copy(band_down, down_band, load_sem.at[7]),
+        pltpu.make_async_copy(coef_hbm, coef, load_sem.at[8]),
     ]
-    for load in loads:
+    for load in (loads[2], loads[4], loads[3], loads[0], loads[1]):
         load.start()
-
-    loads[0].wait()
-    loads[1].wait()
-    bucket_id = lax.broadcasted_iota(jnp.int32, (16, own), 0)
-    target = jnp.full((16, own), -1, jnp.int32)
-    for bucket in range(9):
-        tile = (row + bucket // 3 - 1) * cols + col + bucket % 3 - 1
-        target = jnp.where(bucket_id == bucket, tile, target)
-    belongs = target == jnp.broadcast_to(owner_row[...], (16, own))
-    earlier = (
-        lax.broadcasted_iota(jnp.int32, (own, own), 0)
-        < lax.broadcasted_iota(jnp.int32, (own, own), 1)
-    )
-    place = jnp.dot(
-        jnp.where(belongs, 1.0, 0.0), jnp.where(earlier, 1.0, 0.0),
-        preferred_element_type=jnp.float32,
-    )
-    code = lax.broadcasted_iota(jnp.int32, (16, own), 1) + own * (
-        jnp.broadcast_to(offset_row[...], (16, own)) + 1
-    )
-    code = jnp.where(belongs, code.astype(jnp.float32), 0.0)
-    slot_lane = lax.broadcasted_iota(jnp.int32, (16, LANES), 1)
-    filled = jnp.zeros((16, LANES), jnp.float32)
-    for slot in range(CAP):
-        picked = jnp.sum(jnp.where(place == slot, code, 0.0), axis=1, keepdims=True)
-        filled = jnp.where(slot_lane == slot, picked, filled)
-    table[...] = filled.astype(jnp.int32)
-    to_scalar = pltpu.make_async_copy(table, table_scalar, table_sem)
-    to_scalar.start()
 
     def opposite(step):
         return (-step[0], -step[1])
@@ -206,7 +177,7 @@
 
     def label_copy(at):
         return pltpu.make_async_remote_copy(
-            src_ref=table, dst_ref=arrived_table.at[at], send_sem=label_send.at[at],
+            src_ref=rows_out.at[bucket_of(DIRS[at])], dst_ref=arrived_table.at[at], send_sem=label_send.at[at],
             recv_sem=label_recv.at[at], device_id=neighbour(DIRS[at]), device_id_type=MESH,
         )
 
@@ -227,33 +198,79 @@
             packed = jnp.where(lane_group == group, moved, packed)
         strip_out[strip] = packed.astype(jnp.bfloat16)
 
-    def send_slot(slot, carry):
+    def send_pieces(slot, piece_of):
         for at, step in enumerate(DIRS):
-            piece = table_scalar[bucket_of(step), slot] & (own - 1)
-            outgoing[at, slot] = held[piece]
+            outgoing[at, slot] = held[piece_of(bucket_of(step))]
 
             @pl.when(exists(step))
             def _():
                 bucket_copy(at, pl.ds(slot, 1)).start()
-        arrived[len(DIRS), slot] = held[table_scalar[OWN, slot] & (own - 1)]
+        arrived[len(DIRS), slot] = held[piece_of(OWN)]
+
+    def send_slot(slot, carry):
+        send_pieces(slot, lambda bucket: table_scalar[bucket, slot] & (own - 1))
         return carry
 
     loads[2].wait()
-    loads[3].wait()
-    pack_strip(0, side, LANES - HALO)
-    pack_strip(1, LANES, 0)
+    bucket_id = lax.broadcasted_iota(jnp.int32, (16, own), 0)
+    target = jnp.full((16, own), -1, jnp.int32)
+    for bucket in range(9):
+        tile = (row + bucket // 3 - 1) * cols + col + bucket % 3 - 1
+        target = jnp.where(bucket_id == bucket, tile, target)
+    belongs = target == jnp.broadcast_to(owner_row[...], (16, own))
+    number = lax.broadcasted_iota(jnp.int32, (16, own), 1).astype(jnp.float32)
+    leader = [
+        jnp.min(jnp.where(belongs & (bucket_id == bucket), number, own - 1.0)).astype(jnp.int32)
+        & (own - 1)
+        for bucket in range(9)
+    ]
     tall_group = 3 - jnp.where(row == 0, 1, 0) - jnp.where(row == rows - 1, 1, 0)
     wide_group = 3 - jnp.where(col == 0, 1, 0) - jnp.where(col == cols - 1, 1, 0)
     pl.semaphore_wait(barrier, tall_group * wide_group - 1)
+    loads[4].wait()
+    send_pieces(0, lambda bucket: leader[bucket])
+
+    loads[3].wait()
+    earlier = (
+        lax.broadcasted_iota(jnp.int32, (own, own), 0)
+        < lax.broadcasted_iota(jnp.int32, (own, own), 1)
+    )
+    place = jnp.dot(
+        jnp.where(belongs, 1.0, 0.0), jnp.where(earlier, 1.0, 0.0),
+        preferred_element_type=jnp.float32,
+    )
+    code = lax.broadcasted_iota(jnp.int32, (16, own), 1) + own * (
+        jnp.broadcast_to(offset_row[...], (16, own)) + 1
+    )
+    code = jnp.where(belongs, code.astype(jnp.float32), 0.0)
+    slot_lane = lax.broadcasted_iota(jnp.int32, (16, LANES), 1)
+    filled = jnp.zeros((16, LANES), jnp.float32)
+    for slot in range(CAP):
+        picked = jnp.sum(jnp.where(place == slot, code, 0.0), axis=1, keepdims=True)
+        filled = jnp.where(slot_lane == slot, picked, filled)
+    filled = filled.astype(jnp.int32)
+    table[...] = filled
+    for bucket in range(9):
+        rows_out[bucket] = filled[bucket : bucket + 1]
+    to_scalar = pltpu.make_async_copy(table, table_scalar, table_sem)
+    to_scalar.start()
+
+    loads[0].wait()
+    loads[1].wait()
+    pack_strip(0, side, LANES - HALO)
+    pack_strip(1, LANES, 0)
     for at, step in enumerate(DIRS):
         @pl.when(exists(step))
         def _():
             rim_copy(at).start()
             label_copy(at).start()
-    loads[4].wait()
     to_scalar.wait()
-    lax.fori_loop(0, CAP, send_slot, 0)
-
+    lax.fori_loop(1, 4, send_slot, 0)
+    for load in loads[5:]:
+        load.start()
+    lax.fori_loop(4, CAP, send_slot, 0)
+
+    loads[8].wait()
     lane = lax.broadcasted_iota(jnp.int32, (8, side), 1)
     u = ((col * side + lane).astype(jnp.float32) + 0.5) * (2.0 / (side * cols)) - 1.0
     for basis in range(BASES):
@@ -263,7 +280,7 @@
                 total = total * u + coef[basis, term_powers.index((power_u, power_v))]
             inner[basis, power_v] = total
 
-    for load in loads[5:]:
+    for load in loads[5:8]:
         load.wait()
     wide = padded.shape[1]
 
@@ -356,9 +373,9 @@
         @pl.when(exists(opposite(step)))
         def _():
             label_copy(at).wait_recv()
-            tags[pl.ds(at, 1)] = arrived_table[at, pl.ds(bucket_of(step), 1)]
+            tags[pl.ds(at, 1)] = arrived_table[at]
     tags[pl.ds(len(DIRS), 1)] = table[pl.ds(OWN, 1)]
-    sort_plan(own, side // LANES, tags, plan, share)
+    sort_plan(own, side // LANES, tags, plan)
 
     for at, step in enumerate(DIRS):
         @pl.when(exists(step))
@@ -372,7 +389,7 @@
             bucket_copy(at).wait_recv()
 
 
-def join_kernel(plan, share, arrived, matched, out, total, out_sem):
+def join_kernel(plan, arrived, matched, out, total, out_sem):
     side = out.shape[1]
     per_row = side // LANES
 
@@ -384,7 +401,7 @@
         return pltpu.make_async_copy(total.at[lines], out.at[lines], out_sem.at[block_row])
 
     def join_row(block_row, start):
-        end = plan[2, block_row]
+        end = plan[3, block_row]
         lines = row_lines(block_row)
 
         def add(at, carry):
@@ -392,7 +409,9 @@
             column = pl.multiple_of((plan[1, at] - block_row * per_row) * LANES, LANES)
             columns = pl.ds(column, LANES)
             piece = arrived[lax.div(slot, CAP), slot & (CAP - 1)].astype(jnp.float32)
-            total[lines, columns] = total[lines, columns] + share[2, at] * piece
+            share = 1.0 / jnp.full((8, LANES), jnp.maximum(plan[2, at], 1).astype(jnp.float32))
+            share = jnp.tile(share, (LANES // 8, 1))
+            total[lines, columns] = total[lines, columns] + share * piece
             return carry
 
         lax.fori_loop(start, end, add, 0)
@@ -415,23 +434,24 @@
     band_across, band_down = band_tables()
     tall = side + 2 * HALO
     dma = pltpu.SemaphoreType.DMA
-    arrived, plan, share, matched = pl.pallas_call(
+    arrived, plan, matched = pl.pallas_call(
         send_kernel,
         out_shape=[
             jax.ShapeDtypeStruct((count + 1, CAP, block_side, block_side), jnp.bfloat16),
             jax.ShapeDtypeStruct((8, 2 * LANES), jnp.int32),
-            jax.ShapeDtypeStruct((8, 2 * LANES), jnp.float32),
             jax.ShapeDtypeStruct((side, side), jnp.float32),
         ],
-        in_specs=[hbm, hbm, smem, hbm, hbm, hbm, hbm],
-        out_specs=[vmem, vmem, vmem, vmem],
+        in_specs=[hbm] * 7,
+        out_specs=[vmem, vmem, vmem],
         scratch_shapes=[
             pltpu.VMEM((own, block_side, block_side), jnp.bfloat16),
+            pltpu.SMEM(coefficients.shape, jnp.float32),
             pltpu.VMEM((1, own), jnp.int32),
             pltpu.VMEM((1, own), jnp.int32),
             pltpu.VMEM((16, LANES), jnp.int32),
+            pltpu.VMEM((9, 1, LANES), jnp.int32),
             pltpu.SMEM((16, LANES), jnp.int32),
-            pltpu.VMEM((count, 16, LANES), jnp.int32),
+            pltpu.VMEM((count, 1, LANES), jnp.int32),
             pltpu.VMEM((16, LANES), jnp.int32),
             pltpu.VMEM((count, CAP, block_side, block_side), jnp.bfloat16),
             pltpu.VMEM((tall, side + 2 * LANES), jnp.bfloat16),
@@ -441,7 +461,7 @@
             pltpu.VMEM((BASES, DEGREE + 1, 8, side), jnp.float32),
             pltpu.VMEM(band_across.shape, jnp.bfloat16),
             pltpu.VMEM(band_down.shape, jnp.bfloat16),
-            dma((8,)), dma, dma((count,)), dma((count,)), dma((count,)), dma((count,)),
+            dma((9,)), dma, dma((count,)), dma((count,)), dma((count,)), dma((count,)),
             dma((count,)), dma((count,)),
         ],
         compiler_params=pltpu.CompilerParams(
@@ -460,13 +480,13 @@
     joined, _ = pl.pallas_call(
         join_kernel,
         out_shape=[jax.ShapeDtypeStruct((side, side), jnp.float32)] * 2,
-        in_specs=[smem, smem, vmem, vmem],
+        in_specs=[smem, vmem, vmem],
         out_specs=[hbm, vmem],
-        input_output_aliases={3: 1},
+        input_output_aliases={2: 1},
         scratch_shapes=[dma((side // block_side,))],
         compiler_params=pltpu.CompilerParams(vmem_limit_bytes=32 << 20),
         name="join",
-    )(plan, share, arrived, matched)
+    )(plan, arrived, matched)
     return joined
 
 

time: 46.1 us -> 44.9 us (0.974)
  Pallas kernels: 45.8 us -> 44.3 us
    pallas_call x1, Pallas kernels: 42.8 us -> 41.4 us  [on_device(): pl.pallas_call(send_kernel, out_shape=[jax.ShapeDtypeStruct((count + 1, C...]
where the time goes in v4:
time: 44.9 us; the launch traced here: 44.3 us
  Pallas kernels  44.3 us (99%)
    pallas_call x1, Pallas kernels, on_device(): pl.pallas_call(send_kernel, out_shape=[jax.ShapeDtypeStruct((count + 1, C...  41.4 us
    pallas_call x1, Pallas kernels, on_device(): pl.pallas_call(join_kernel, out_shape=[jax.ShapeDtypeStruct((side, side),...  2.88 us

profile of v4, /device:TPU:105, one launch (start us, length us, event | category | flops | bytes accessed | tf_op | source)
XLA Modules:
  0.0 44.3 jit_solution(4212277434270742784)
XLA Ops:
  0.0 41.4 %send.1 = (bf16[9,16,128,128]{3,2,1,0:T(8,128)(2,1)S(1)}, s32[8,256]{1,0:T(8,128)S(1)}, f32[1024,1024]{1,0:T(8,128)S(1)}) custom-call(s32[1,64]{1,0:T(1,128)} %bitcast.2, s32[1,64]{1,0:T(1,128)} %bitcast.3, f32[3,15]{1,0:T(4,128)} %coef_hbm.1, bf16[64,128,128]{2,1,0:T(8,128)(2,1)} %pieces.1, bf16[1024,1024]{1,0:T(8,128)(2,1)} %template.1, ...), custom_call_target="tpu_custom_call" | custom-call | tf_op jit(solution)/shard_map/send/pallas_call | solution.py:437
  41.4 2.9 %join.1 = (f32[1024,1024]{1,0:T(8,128)}, f32[1024,1024]{1,0:T(8,128)S(1)}) custom-call(s32[8,256]{1,0:T(8,128)S(1)} %get-tuple-element.9.plan, bf16[9,16,128,128]{3,2,1,0:T(8,128)(2,1)S(1)} %get-tuple-element.10.arrived, f32[1024,1024]{1,0:T(8,128)S(1)} %get-tuple-element.11.matched), custom_call_target="tpu_custom_call", output_to_operand_aliasing={{1}: (2, {})} | custom-call | tf_op jit(solution)/shard_map/join/pallas_call | solution.py:480

commit v5 on v4

--- a/solution.py
+++ b/solution.py
@@ -18,6 +18,9 @@
 term_powers = [(degree - power_v, power_v) for degree in range(5) for power_v in range(degree + 1)]
 
 DIRS = ((1, 1), (-1, -1), (1, -1), (-1, 1), (0, 1), (0, -1), (1, 0), (-1, 0))
+DIAGONALS = 4
+RELAYED = 8
+EARLY = 12
 OWN = 4
 MESH = pl.DeviceIdType.MESH
 
@@ -109,7 +112,8 @@
     arrived, plan, matched,
     held, coef, owner_row, offset_row, table, rows_out, table_scalar, arrived_table,
     tags, outgoing, padded, strip_out, strip_in, across, inner, row_band, down_band,
-    load_sem, table_sem, send_sem, recv_sem, label_send, label_recv, rim_send, rim_recv,
+    relay, load_sem, table_sem, send_sem, recv_sem, label_send, label_recv, rim_send, rim_recv,
+    relay_recv, onward_send,
 ):
     rows, cols = lax.axis_size("py"), lax.axis_size("px")
     row, col = lax.axis_index("py"), lax.axis_index("px")
@@ -198,17 +202,67 @@
             packed = jnp.where(lane_group == group, moved, packed)
         strip_out[strip] = packed.astype(jnp.bfloat16)
 
-    def send_pieces(slot, piece_of):
+    def column_first(step):
+        return row == (2 if step[0] < 0 else rows - 3)
+
+    def row_first(step):
+        return row == (1 if step[0] > 0 else rows - 2)
+
+    def relay_copy(at, slots):
+        step = DIRS[at]
+        return pltpu.make_async_remote_copy(
+            src_ref=outgoing.at[at, slots], dst_ref=relay.at[at, slots],
+            send_sem=send_sem.at[at], recv_sem=relay_recv.at[at],
+            device_id=(
+                row + jnp.where(row_first(step), 0, step[0]),
+                col + jnp.where(column_first(step), 0, step[1]),
+            ),
+            device_id_type=MESH,
+        )
+
+    def turns_column(step):
+        return row == (1 if step[0] < 0 else rows - 2)
+
+    def turns_row(step):
+        return row == (1 if step[0] > 0 else rows - 2)
+
+    def turns(step):
+        ahead, behind = col + step[1], col - step[1]
+        return (turns_column(step) & (ahead >= 0) & (ahead < cols)) | (
+            turns_row(step) & (behind >= 0) & (behind < cols)
+        )
+
+    def onward_copy(at, slots):
+        step = DIRS[at]
+        return pltpu.make_async_remote_copy(
+            src_ref=relay.at[at, slots], dst_ref=arrived.at[at, slots],
+            send_sem=onward_send.at[at], recv_sem=recv_sem.at[at],
+            device_id=(
+                row + jnp.where(turns_row(step), step[0], 0),
+                col + jnp.where(turns_column(step), step[1], 0),
+            ),
+            device_id_type=MESH,
+        )
+
+    def send_pieces(slot, piece_of, relayed):
         for at, step in enumerate(DIRS):
             outgoing[at, slot] = held[piece_of(bucket_of(step))]
-
-            @pl.when(exists(step))
+            direct = exists(step)
+            if relayed and at < DIAGONALS:
+                turned = column_first(step) | row_first(step)
+
+                @pl.when(direct & turned)
+                def _():
+                    relay_copy(at, pl.ds(slot, 1)).start()
+                direct = direct & jnp.logical_not(turned)
+
+            @pl.when(direct)
             def _():
                 bucket_copy(at, pl.ds(slot, 1)).start()
         arrived[len(DIRS), slot] = held[piece_of(OWN)]
 
-    def send_slot(slot, carry):
-        send_pieces(slot, lambda bucket: table_scalar[bucket, slot] & (own - 1))
+    def send_slot(relayed, slot, carry):
+        send_pieces(slot, lambda bucket: table_scalar[bucket, slot] & (own - 1), relayed)
         return carry
 
     loads[2].wait()
@@ -228,7 +282,7 @@
     wide_group = 3 - jnp.where(col == 0, 1, 0) - jnp.where(col == cols - 1, 1, 0)
     pl.semaphore_wait(barrier, tall_group * wide_group - 1)
     loads[4].wait()
-    send_pieces(0, lambda bucket: leader[bucket])
+    send_pieces(0, lambda bucket: leader[bucket], True)
 
     loads[3].wait()
     earlier = (
@@ -265,10 +319,11 @@
             rim_copy(at).start()
             label_copy(at).start()
     to_scalar.wait()
-    lax.fori_loop(1, 4, send_slot, 0)
+    lax.fori_loop(1, 4, functools.partial(send_slot, True), 0)
     for load in loads[5:]:
         load.start()
-    lax.fori_loop(4, CAP, send_slot, 0)
+    lax.fori_loop(4, RELAYED, functools.partial(send_slot, True), 0)
+    lax.fori_loop(RELAYED, EARLY, functools.partial(send_slot, False), 0)
 
     loads[8].wait()
     lane = lax.broadcasted_iota(jnp.int32, (8, side), 1)
@@ -367,6 +422,18 @@
 
     lax.fori_loop(0, blocks, column_pass, 0)
 
+    for at in range(DIAGONALS):
+        @pl.when(turns(DIRS[at]))
+        def _():
+            relay_copy(at, pl.ds(0, RELAYED)).wait_recv()
+
+            def pass_on(slot, carry):
+                onward_copy(at, pl.ds(slot, 1)).start()
+                return carry
+
+            lax.fori_loop(0, RELAYED, pass_on, 0)
+    lax.fori_loop(EARLY, CAP, functools.partial(send_slot, False), 0)
+
     for at, step in enumerate(DIRS):
         tags[pl.ds(at, 1)] = jnp.zeros((1, LANES), jnp.int32)
 
@@ -377,6 +444,10 @@
     tags[pl.ds(len(DIRS), 1)] = table[pl.ds(OWN, 1)]
     sort_plan(own, side // LANES, tags, plan)
 
+    for at in range(DIAGONALS):
+        @pl.when(turns(DIRS[at]))
+        def _():
+            onward_copy(at, pl.ds(0, RELAYED)).wait_send()
     for at, step in enumerate(DIRS):
         @pl.when(exists(step))
         def _():
@@ -461,8 +532,9 @@
             pltpu.VMEM((BASES, DEGREE + 1, 8, side), jnp.float32),
             pltpu.VMEM(band_across.shape, jnp.bfloat16),
             pltpu.VMEM(band_down.shape, jnp.bfloat16),
+            pltpu.VMEM((DIAGONALS, RELAYED, block_side, block_side), jnp.bfloat16),
             dma((9,)), dma, dma((count,)), dma((count,)), dma((count,)), dma((count,)),
-            dma((count,)), dma((count,)),
+            dma((count,)), dma((count,)), dma((DIAGONALS,)), dma((DIAGONALS,)),
         ],
         compiler_params=pltpu.CompilerParams(
             collective_id=0, has_side_effects=True, vmem_limit_bytes=40 << 20

time: 44.9 us -> 43.5 us (0.969)
  Pallas kernels: 44.3 us -> 42.9 us
    pallas_call x1, Pallas kernels: 41.4 us -> 39.8 us  [on_device(): pl.pallas_call(send_kernel, out_shape=[jax.ShapeDtypeStruct((count + 1, C...]
where the time goes in v5:
time: 43.5 us; the launch traced here: 42.9 us
  Pallas kernels  42.9 us (99%)
    pallas_call x1, Pallas kernels, on_device(): pl.pallas_call(send_kernel, out_shape=[jax.ShapeDtypeStruct((count + 1, C...  39.8 us
    pallas_call x1, Pallas kernels, on_device(): pl.pallas_call(join_kernel, out_shape=[jax.ShapeDtypeStruct((side, side),...  3.13 us

profile of v5, /device:TPU:105, one launch (start us, length us, event | category | flops | bytes accessed | tf_op | source)
XLA Modules:
  0.0 42.9 jit_solution(7497725726798573598)
XLA Ops:
  0.0 39.8 %send.1 = (bf16[9,16,128,128]{3,2,1,0:T(8,128)(2,1)S(1)}, s32[8,256]{1,0:T(8,128)S(1)}, f32[1024,1024]{1,0:T(8,128)S(1)}) custom-call(s32[1,64]{1,0:T(1,128)} %bitcast.2, s32[1,64]{1,0:T(1,128)} %bitcast.3, f32[3,15]{1,0:T(4,128)} %coef_hbm.1, bf16[64,128,128]{2,1,0:T(8,128)(2,1)} %pieces.1, bf16[1024,1024]{1,0:T(8,128)(2,1)} %template.1, ...), custom_call_target="tpu_custom_call" | custom-call | tf_op jit(solution)/shard_map/send/pallas_call | solution.py:508
  39.8 3.1 %join.1 = (f32[1024,1024]{1,0:T(8,128)}, f32[1024,1024]{1,0:T(8,128)S(1)}) custom-call(s32[8,256]{1,0:T(8,128)S(1)} %get-tuple-element.9.plan, bf16[9,16,128,128]{3,2,1,0:T(8,128)(2,1)S(1)} %get-tuple-element.10.arrived, f32[1024,1024]{1,0:T(8,128)S(1)} %get-tuple-element.11.matched), custom_call_target="tpu_custom_call", output_to_operand_aliasing={{1}: (2, {})} | custom-call | tf_op jit(solution)/shard_map/join/pallas_call | solution.py:552

commit v6 on v5

--- a/solution.py
+++ b/solution.py
@@ -20,7 +20,6 @@
 DIRS = ((1, 1), (-1, -1), (1, -1), (-1, 1), (0, 1), (0, -1), (1, 0), (-1, 0))
 DIAGONALS = 4
 RELAYED = 8
-EARLY = 12
 OWN = 4
 MESH = pl.DeviceIdType.MESH
 
@@ -51,7 +50,7 @@
     return across, down
 
 
-def sort_plan(own, per_row, tags, plan):
+def sort_plan(own, per_row, tags, plan, share):
     count = len(DIRS)
     blocks = per_row * per_row
     shape = (blocks, LANES)
@@ -105,11 +104,13 @@
         )
     wide_line = lax.broadcasted_iota(jnp.int32, listed.shape, 0)
     plan[...] = jnp.where(wide_line == 3, ends, listed).astype(jnp.int32)
+    share[...] = 1.0 / jnp.maximum(listed, 1.0)
 
 
 def send_kernel(
     owner, offset, coef_hbm, pieces, template, band_across, band_down,
-    arrived, plan, matched,
+    arrived, plan_scalar, share_scalar, matched,
+    plan, share,
     held, coef, owner_row, offset_row, table, rows_out, table_scalar, arrived_table,
     tags, outgoing, padded, strip_out, strip_in, across, inner, row_band, down_band,
     relay, load_sem, table_sem, send_sem, recv_sem, label_send, label_recv, rim_send, rim_recv,
@@ -323,7 +324,7 @@
     for load in loads[5:]:
         load.start()
     lax.fori_loop(4, RELAYED, functools.partial(send_slot, True), 0)
-    lax.fori_loop(RELAYED, EARLY, functools.partial(send_slot, False), 0)
+    lax.fori_loop(RELAYED, CAP, functools.partial(send_slot, False), 0)
 
     loads[8].wait()
     lane = lax.broadcasted_iota(jnp.int32, (8, side), 1)
@@ -432,7 +433,6 @@
                 return carry
 
             lax.fori_loop(0, RELAYED, pass_on, 0)
-    lax.fori_loop(EARLY, CAP, functools.partial(send_slot, False), 0)
 
     for at, step in enumerate(DIRS):
         tags[pl.ds(at, 1)] = jnp.zeros((1, LANES), jnp.int32)
@@ -442,7 +442,13 @@
             label_copy(at).wait_recv()
             tags[pl.ds(at, 1)] = arrived_table[at]
     tags[pl.ds(len(DIRS), 1)] = table[pl.ds(OWN, 1)]
-    sort_plan(own, side // LANES, tags, plan)
+    sort_plan(own, side // LANES, tags, plan, share)
+    plan_copies = [
+        pltpu.make_async_copy(plan, plan_scalar, load_sem.at[0]),
+        pltpu.make_async_copy(share, share_scalar, load_sem.at[1]),
+    ]
+    for plan_copy in plan_copies:
+        plan_copy.start()
 
     for at in range(DIAGONALS):
         @pl.when(turns(DIRS[at]))
@@ -458,9 +464,11 @@
         @pl.when(exists(opposite(step)))
         def _():
             bucket_copy(at).wait_recv()
-
-
-def join_kernel(plan, arrived, matched, out, total, out_sem):
+    for plan_copy in plan_copies:
+        plan_copy.wait()
+
+
+def join_kernel(plan, share, arrived, matched, out, total, out_sem):
     side = out.shape[1]
     per_row = side // LANES
 
@@ -480,9 +488,7 @@
             column = pl.multiple_of((plan[1, at] - block_row * per_row) * LANES, LANES)
             columns = pl.ds(column, LANES)
             piece = arrived[lax.div(slot, CAP), slot & (CAP - 1)].astype(jnp.float32)
-            share = 1.0 / jnp.full((8, LANES), jnp.maximum(plan[2, at], 1).astype(jnp.float32))
-            share = jnp.tile(share, (LANES // 8, 1))
-            total[lines, columns] = total[lines, columns] + share * piece
+            total[lines, columns] = total[lines, columns] + share[2, at] * piece
             return carry
 
         lax.fori_loop(start, end, add, 0)
@@ -505,16 +511,19 @@
     band_across, band_down = band_tables()
     tall = side + 2 * HALO
     dma = pltpu.SemaphoreType.DMA
-    arrived, plan, matched = pl.pallas_call(
+    arrived, plan, share, matched = pl.pallas_call(
         send_kernel,
         out_shape=[
             jax.ShapeDtypeStruct((count + 1, CAP, block_side, block_side), jnp.bfloat16),
-            jax.ShapeDtypeStruct((8, 2 * LANES), jnp.int32),
+            pltpu.SMEM((8, 2 * LANES), jnp.int32),
+            pltpu.SMEM((8, 2 * LANES), jnp.float32),
             jax.ShapeDtypeStruct((side, side), jnp.float32),
         ],
         in_specs=[hbm] * 7,
-        out_specs=[vmem, vmem, vmem],
+        out_specs=[vmem, smem, smem, vmem],
         scratch_shapes=[
+            pltpu.VMEM((8, 2 * LANES), jnp.int32),
+            pltpu.VMEM((8, 2 * LANES), jnp.float32),
             pltpu.VMEM((own, block_side, block_side), jnp.bfloat16),
             pltpu.SMEM(coefficients.shape, jnp.float32),
             pltpu.VMEM((1, own), jnp.int32),
@@ -552,13 +561,13 @@
     joined, _ = pl.pallas_call(
         join_kernel,
         out_shape=[jax.ShapeDtypeStruct((side, side), jnp.float32)] * 2,
-        in_specs=[smem, vmem, vmem],
+        in_specs=[smem, smem, vmem, vmem],
         out_specs=[hbm, vmem],
-        input_output_aliases={2: 1},
+        input_output_aliases={3: 1},
         scratch_shapes=[dma((side // block_side,))],
         compiler_params=pltpu.CompilerParams(vmem_limit_bytes=32 << 20),
         name="join",
-    )(plan, arrived, matched)
+    )(plan, share, arrived, matched)
     return joined
 
 

time: 43.5 us -> 42.4 us (0.975)
  Pallas kernels: 42.9 us -> 41.7 us
    pallas_call x1, Pallas kernels: 3.13 us -> 2.24 us  [on_device(): pl.pallas_call(join_kernel, out_shape=[jax.ShapeDtypeStruct((side, side),...]
where the time goes in v6:
time: 42.4 us; the launch traced here: 41.7 us
  Pallas kernels  41.7 us (98%)
    pallas_call x1, Pallas kernels, on_device(): pl.pallas_call(send_kernel, out_shape=[jax.ShapeDtypeStruct((count + 1, C...  39.5 us
    pallas_call x1, Pallas kernels, on_device(): pl.pallas_call(join_kernel, out_shape=[jax.ShapeDtypeStruct((side, side),...  2.24 us

profile of v6, /device:TPU:105, one launch (start us, length us, event | category | flops | bytes accessed | tf_op | source)
XLA Modules:
  0.0 41.7 jit_solution(2159562843686595296)
XLA Ops:
  0.0 39.5 %send.1 = (bf16[9,16,128,128]{3,2,1,0:T(8,128)(2,1)S(1)}, s32[8,256]{1,0:T(8,128)S(4)}, f32[8,256]{1,0:T(8,128)S(4)}, f32[1024,1024]{1,0:T(8,128)S(1)}) custom-call(s32[1,64]{1,0:T(1,128)} %bitcast.2, s32[1,64]{1,0:T(1,128)} %bitcast.3, f32[3,15]{1,0:T(4,128)} %coef_hbm.1, bf16[64,128,128]{2,1,0:T(8,128)(2,1)} %pieces.1, bf16[1024,1024]{1,0:T(8,128)(2,1)} %template.1, ...), custom_call_target="tpu_custom_call" | custom-call | tf_op jit(solution)/shard_map/send/pallas_call | solution.py:514
  39.5 2.2 %join.1 = (f32[1024,1024]{1,0:T(8,128)}, f32[1024,1024]{1,0:T(8,128)S(1)}) custom-call(s32[8,256]{1,0:T(8,128)S(4)} %get-tuple-element.10.plan, f32[8,256]{1,0:T(8,128)S(4)} %get-tuple-element.11.share, bf16[9,16,128,128]{3,2,1,0:T(8,128)(2,1)S(1)} %get-tuple-element.12.arrived, ...), custom_call_target="tpu_custom_call", output_to_operand_aliasing={{1}: (3, {})} | custom-call | tf_op jit(solution)/shard_map/join/pallas_call | solution.py:561

commit v7 on v6

--- a/solution.py
+++ b/solution.py
@@ -20,6 +20,9 @@
 DIRS = ((1, 1), (-1, -1), (1, -1), (-1, 1), (0, 1), (0, -1), (1, 0), (-1, 0))
 DIAGONALS = 4
 RELAYED = 8
+PLANE = 4
+DETOUR = 3
+EARLY = 12
 OWN = 4
 MESH = pl.DeviceIdType.MESH
 
@@ -114,7 +117,7 @@
     held, coef, owner_row, offset_row, table, rows_out, table_scalar, arrived_table,
     tags, outgoing, padded, strip_out, strip_in, across, inner, row_band, down_band,
     relay, load_sem, table_sem, send_sem, recv_sem, label_send, label_recv, rim_send, rim_recv,
-    relay_recv, onward_send,
+    relay_recv, onward_send, detour, detour_recv, detour_send,
 ):
     rows, cols = lax.axis_size("py"), lax.axis_size("px")
     row, col = lax.axis_index("py"), lax.axis_index("px")
@@ -129,11 +132,28 @@
     def neighbour(step):
         return (row + step[0], col + step[1])
 
+    plane = lax.div(col, PLANE)
+    planes = cols // PLANE
+    leads = col - plane * PLANE == 0
+    trails = col - plane * PLANE == PLANE - 1
+
     barrier = pltpu.get_barrier_semaphore()
     for step in DIRS:
         @pl.when(exists(step))
         def _():
             pl.semaphore_signal(barrier, inc=1, device_id=neighbour(step), device_id_type=MESH)
+
+    for far, there in (
+        (PLANE - 1, leads),
+        (1 - PLANE, trails),
+        (PLANE, (leads | trails) & (plane < planes - 1)),
+        (-PLANE, (leads | trails) & (plane > 0)),
+    ):
+        @pl.when(there)
+        def _():
+            pl.semaphore_signal(
+                barrier, inc=1, device_id=(row, col + far), device_id_type=MESH
+            )
 
     body = padded.at[pl.ds(HALO, side)]
     loads = [
@@ -245,6 +265,29 @@
             device_id_type=MESH,
         )
 
+    detours = (
+        (DIRS.index((0, 1)), 1, trails & (plane < planes - 1), DETOUR * (plane + 1)),
+        (DIRS.index((0, -1)), -1, leads & (plane > 0), DETOUR * (planes - plane)),
+    )
+    passes = (
+        (DIRS.index((0, 1)), 1, trails, plane),
+        (DIRS.index((0, -1)), -1, leads, planes - 1 - plane),
+    )
+
+    def detour_copy(at, way, slots):
+        return pltpu.make_async_remote_copy(
+            src_ref=outgoing.at[at, slots], dst_ref=detour.at[slots],
+            send_sem=send_sem.at[at], recv_sem=detour_recv,
+            device_id=(row, col + way * PLANE), device_id_type=MESH,
+        )
+
+    def rejoin_copy(at, way, slots):
+        return pltpu.make_async_remote_copy(
+            src_ref=detour.at[slots], dst_ref=arrived.at[at, slots],
+            send_sem=detour_send, recv_sem=recv_sem.at[at],
+            device_id=(row, col - way * (PLANE - 1)), device_id_type=MESH,
+        )
+
     def send_pieces(slot, piece_of, relayed):
         for at, step in enumerate(DIRS):
             outgoing[at, slot] = held[piece_of(bucket_of(step))]
@@ -256,6 +299,14 @@
                 def _():
                     relay_copy(at, pl.ds(slot, 1)).start()
                 direct = direct & jnp.logical_not(turned)
+            for detour_at, way, here, slots in detours:
+                if at == detour_at:
+                    around = here & (slot < slots)
+
+                    @pl.when(around)
+                    def _():
+                        detour_copy(at, way, pl.ds(slot, 1)).start()
+                    direct = direct & jnp.logical_not(around)
 
             @pl.when(direct)
             def _():
@@ -281,7 +332,9 @@
     ]
     tall_group = 3 - jnp.where(row == 0, 1, 0) - jnp.where(row == rows - 1, 1, 0)
     wide_group = 3 - jnp.where(col == 0, 1, 0) - jnp.where(col == cols - 1, 1, 0)
-    pl.semaphore_wait(barrier, tall_group * wide_group - 1)
+    mates = 3 - jnp.where(plane == 0, 1, 0) - jnp.where(plane == planes - 1, 1, 0)
+    mates = jnp.where(leads | trails, mates, 0)
+    pl.semaphore_wait(barrier, tall_group * wide_group - 1 + mates)
     loads[4].wait()
     send_pieces(0, lambda bucket: leader[bucket], True)
 
@@ -324,7 +377,7 @@
     for load in loads[5:]:
         load.start()
     lax.fori_loop(4, RELAYED, functools.partial(send_slot, True), 0)
-    lax.fori_loop(RELAYED, CAP, functools.partial(send_slot, False), 0)
+    lax.fori_loop(RELAYED, EARLY, functools.partial(send_slot, False), 0)
 
     loads[8].wait()
     lane = lax.broadcasted_iota(jnp.int32, (8, side), 1)
@@ -433,6 +486,18 @@
                 return carry
 
             lax.fori_loop(0, RELAYED, pass_on, 0)
+    for at, way, here, share_of in passes:
+        for thirds in range(1, planes):
+            @pl.when(here & (share_of == thirds))
+            def _():
+                detour_copy(at, way, pl.ds(0, DETOUR * thirds)).wait_recv()
+
+                def rejoin(slot, carry):
+                    rejoin_copy(at, way, pl.ds(slot, 1)).start()
+                    return carry
+
+                lax.fori_loop(0, DETOUR * thirds, rejoin, 0)
+    lax.fori_loop(EARLY, CAP, functools.partial(send_slot, False), 0)
 
     for at, step in enumerate(DIRS):
         tags[pl.ds(at, 1)] = jnp.zeros((1, LANES), jnp.int32)
@@ -454,6 +519,11 @@
         @pl.when(turns(DIRS[at]))
         def _():
             onward_copy(at, pl.ds(0, RELAYED)).wait_send()
+    for at, way, here, share_of in passes:
+        for thirds in range(1, planes):
+            @pl.when(here & (share_of == thirds))
+            def _():
+                rejoin_copy(at, way, pl.ds(0, DETOUR * thirds)).wait_send()
     for at, step in enumerate(DIRS):
         @pl.when(exists(step))
         def _():
@@ -544,6 +614,7 @@
             pltpu.VMEM((DIAGONALS, RELAYED, block_side, block_side), jnp.bfloat16),
             dma((9,)), dma, dma((count,)), dma((count,)), dma((count,)), dma((count,)),
             dma((count,)), dma((count,)), dma((DIAGONALS,)), dma((DIAGONALS,)),
+            pltpu.VMEM((3 * DETOUR, block_side, block_side), jnp.bfloat16), dma, dma,
         ],
         compiler_params=pltpu.CompilerParams(
             collective_id=0, has_side_effects=True, vmem_limit_bytes=40 << 20

time: 42.4 us -> 40.9 us (0.965); the launches traced: 41.7 us -> 40.7 us
  Pallas kernels: 41.7 us -> 40.7 us
    pallas_call x1, Pallas kernels: 39.5 us -> 38.4 us  [on_device(): pl.pallas_call(send_kernel, out_shape=[jax.ShapeDtypeStruct((count + 1, C...]
where the time goes in v7:
time: 40.9 us; the launch traced here: 40.7 us
  Pallas kernels  40.7 us (100%)
    pallas_call x1, Pallas kernels, on_device(): pl.pallas_call(send_kernel, out_shape=[jax.ShapeDtypeStruct((count + 1, C...  38.4 us
    pallas_call x1, Pallas kernels, on_device(): pl.pallas_call(join_kernel, out_shape=[jax.ShapeDtypeStruct((side, side),...  2.24 us

profile of v7, /device:TPU:105, one launch (start us, length us, event | category | flops | bytes accessed | tf_op | source)
XLA Modules:
  0.0 40.7 jit_solution(2885716558218695302)
XLA Ops:
  0.0 38.4 %send.1 = (bf16[9,16,128,128]{3,2,1,0:T(8,128)(2,1)S(1)}, s32[8,256]{1,0:T(8,128)S(4)}, f32[8,256]{1,0:T(8,128)S(4)}, f32[1024,1024]{1,0:T(8,128)S(1)}) custom-call(s32[1,64]{1,0:T(1,128)} %bitcast.2, s32[1,64]{1,0:T(1,128)} %bitcast.3, f32[3,15]{1,0:T(4,128)} %coef_hbm.1, bf16[64,128,128]{2,1,0:T(8,128)(2,1)} %pieces.1, bf16[1024,1024]{1,0:T(8,128)(2,1)} %template.1, ...), custom_call_target="tpu_custom_call" | custom-call | tf_op jit(solution)/shard_map/send/pallas_call | solution.py:584
  38.4 2.2 %join.1 = (f32[1024,1024]{1,0:T(8,128)}, f32[1024,1024]{1,0:T(8,128)S(1)}) custom-call(s32[8,256]{1,0:T(8,128)S(4)} %get-tuple-element.10.plan, f32[8,256]{1,0:T(8,128)S(4)} %get-tuple-element.11.share, bf16[9,16,128,128]{3,2,1,0:T(8,128)(2,1)S(1)} %get-tuple-element.12.arrived, ...), custom_call_target="tpu_custom_call", output_to_operand_aliasing={{1}: (3, {})} | custom-call | tf_op jit(solution)/shard_map/join/pallas_call | solution.py:632

commit v8 on v7

--- a/solution.py
+++ b/solution.py
@@ -22,7 +22,7 @@
 RELAYED = 8
 PLANE = 4
 DETOUR = 3
-EARLY = 12
+EARLY = 14
 OWN = 4
 MESH = pl.DeviceIdType.MESH
 

time: 40.9 us -> 40.7 us (level)
  the two profiles are of different devices: /device:TPU:105 before, /device:TPU:107 now
where the time goes in v8:
time: 40.7 us; the launch traced here: 40.5 us
  Pallas kernels  40.5 us (100%)
    pallas_call x1, Pallas kernels, on_device(): pl.pallas_call(send_kernel, out_shape=[jax.ShapeDtypeStruct((count + 1, C...  37.9 us
    pallas_call x1, Pallas kernels, on_device(): pl.pallas_call(join_kernel, out_shape=[jax.ShapeDtypeStruct((side, side),...  2.57 us

profile of v8, /device:TPU:107, one launch (start us, length us, event | category | flops | bytes accessed | tf_op | source)
XLA Modules:
  0.0 40.5 jit_solution(8328907512842360)
XLA Ops:
  0.0 37.9 %send.1 = (bf16[9,16,128,128]{3,2,1,0:T(8,128)(2,1)S(1)}, s32[8,256]{1,0:T(8,128)S(4)}, f32[8,256]{1,0:T(8,128)S(4)}, f32[1024,1024]{1,0:T(8,128)S(1)}) custom-call(s32[1,64]{1,0:T(1,128)} %bitcast.2, s32[1,64]{1,0:T(1,128)} %bitcast.3, f32[3,15]{1,0:T(4,128)} %coef_hbm.1, bf16[64,128,128]{2,1,0:T(8,128)(2,1)} %pieces.1, bf16[1024,1024]{1,0:T(8,128)(2,1)} %template.1, ...), custom_call_target="tpu_custom_call" | custom-call | tf_op jit(solution)/shard_map/send/pallas_call | solution.py:584
  38.0 2.6 %join.1 = (f32[1024,1024]{1,0:T(8,128)}, f32[1024,1024]{1,0:T(8,128)S(1)}) custom-call(s32[8,256]{1,0:T(8,128)S(4)} %get-tuple-element.10.plan, f32[8,256]{1,0:T(8,128)S(4)} %get-tuple-element.11.share, bf16[9,16,128,128]{3,2,1,0:T(8,128)(2,1)S(1)} %get-tuple-element.12.arrived, ...), custom_call_target="tpu_custom_call", output_to_operand_aliasing={{1}: (3, {})} | custom-call | tf_op jit(solution)/shard_map/join/pallas_call | solution.py:632

commit v9 on v8

--- a/solution.py
+++ b/solution.py
@@ -524,18 +524,18 @@
             @pl.when(here & (share_of == thirds))
             def _():
                 rejoin_copy(at, way, pl.ds(0, DETOUR * thirds)).wait_send()
+    for plan_copy in plan_copies:
+        plan_copy.wait()
     for at, step in enumerate(DIRS):
         @pl.when(exists(step))
         def _():
             rim_copy(at).wait_send()
             label_copy(at).wait_send()
             bucket_copy(at).wait_send()
-
-        @pl.when(exists(opposite(step)))
+    for at in reversed(range(len(DIRS))):
+        @pl.when(exists(opposite(DIRS[at])))
         def _():
             bucket_copy(at).wait_recv()
-    for plan_copy in plan_copies:
-        plan_copy.wait()
 
 
 def join_kernel(plan, share, arrived, matched, out, total, out_sem):

time: 40.7 us -> 40.4 us (level)
  the two profiles are of different devices: /device:TPU:107 before, /device:TPU:105 now
where the time goes in v9:
time: 40.4 us; the launch traced here: 39.8 us
  Pallas kernels  39.7 us (98%)
    pallas_call x1, Pallas kernels, on_device(): pl.pallas_call(send_kernel, out_shape=[jax.ShapeDtypeStruct((count + 1, C...  37.4 us
    pallas_call x1, Pallas kernels, on_device(): pl.pallas_call(join_kernel, out_shape=[jax.ShapeDtypeStruct((side, side),...  2.37 us

profile of v9, /device:TPU:105, one launch (start us, length us, event | category | flops | bytes accessed | tf_op | source)
XLA Modules:
  0.0 39.8 jit_solution(2238601443286415408)
XLA Ops:
  0.0 37.4 %send.1 = (bf16[9,16,128,128]{3,2,1,0:T(8,128)(2,1)S(1)}, s32[8,256]{1,0:T(8,128)S(4)}, f32[8,256]{1,0:T(8,128)S(4)}, f32[1024,1024]{1,0:T(8,128)S(1)}) custom-call(s32[1,64]{1,0:T(1,128)} %bitcast.2, s32[1,64]{1,0:T(1,128)} %bitcast.3, f32[3,15]{1,0:T(4,128)} %coef_hbm.1, bf16[64,128,128]{2,1,0:T(8,128)(2,1)} %pieces.1, bf16[1024,1024]{1,0:T(8,128)(2,1)} %template.1, ...), custom_call_target="tpu_custom_call" | custom-call | tf_op jit(solution)/shard_map/send/pallas_call | solution.py:584
  37.4 2.4 %join.1 = (f32[1024,1024]{1,0:T(8,128)}, f32[1024,1024]{1,0:T(8,128)S(1)}) custom-call(s32[8,256]{1,0:T(8,128)S(4)} %get-tuple-element.10.plan, f32[8,256]{1,0:T(8,128)S(4)} %get-tuple-element.11.share, bf16[9,16,128,128]{3,2,1,0:T(8,128)(2,1)S(1)} %get-tuple-element.12.arrived, ...), custom_call_target="tpu_custom_call", output_to_operand_aliasing={{1}: (3, {})} | custom-call | tf_op jit(solution)/shard_map/join/pallas_call | solution.py:632

commit v10 on v9

--- a/solution.py
+++ b/solution.py
@@ -19,7 +19,8 @@
 
 DIRS = ((1, 1), (-1, -1), (1, -1), (-1, 1), (0, 1), (0, -1), (1, 0), (-1, 0))
 DIAGONALS = 4
-RELAYED = 8
+COLUMN_RELAYED = 9
+ROW_RELAYED = 8
 PLANE = 4
 DETOUR = 3
 EARLY = 14
@@ -249,8 +250,9 @@
 
     def turns(step):
         ahead, behind = col + step[1], col - step[1]
-        return (turns_column(step) & (ahead >= 0) & (ahead < cols)) | (
-            turns_row(step) & (behind >= 0) & (behind < cols)
+        return (
+            (turns_column(step) & (ahead >= 0) & (ahead < cols), COLUMN_RELAYED),
+            (turns_row(step) & (behind >= 0) & (behind < cols), ROW_RELAYED),
         )
 
     def onward_copy(at, slots):
@@ -293,7 +295,9 @@
             outgoing[at, slot] = held[piece_of(bucket_of(step))]
             direct = exists(step)
             if relayed and at < DIAGONALS:
-                turned = column_first(step) | row_first(step)
+                turned = (column_first(step) & (slot < COLUMN_RELAYED)) | (
+                    row_first(step) & (slot < ROW_RELAYED)
+                )
 
                 @pl.when(direct & turned)
                 def _():
@@ -376,8 +380,8 @@
     lax.fori_loop(1, 4, functools.partial(send_slot, True), 0)
     for load in loads[5:]:
         load.start()
-    lax.fori_loop(4, RELAYED, functools.partial(send_slot, True), 0)
-    lax.fori_loop(RELAYED, EARLY, functools.partial(send_slot, False), 0)
+    lax.fori_loop(4, COLUMN_RELAYED, functools.partial(send_slot, True), 0)
+    lax.fori_loop(COLUMN_RELAYED, EARLY, functools.partial(send_slot, False), 0)
 
     loads[8].wait()
     lane = lax.broadcasted_iota(jnp.int32, (8, side), 1)
@@ -476,16 +480,6 @@
 
     lax.fori_loop(0, blocks, column_pass, 0)
 
-    for at in range(DIAGONALS):
-        @pl.when(turns(DIRS[at]))
-        def _():
-            relay_copy(at, pl.ds(0, RELAYED)).wait_recv()
-
-            def pass_on(slot, carry):
-                onward_copy(at, pl.ds(slot, 1)).start()
-                return carry
-
-            lax.fori_loop(0, RELAYED, pass_on, 0)
     for at, way, here, share_of in passes:
         for thirds in range(1, planes):
             @pl.when(here & (share_of == thirds))
@@ -497,6 +491,17 @@
                     return carry
 
                 lax.fori_loop(0, DETOUR * thirds, rejoin, 0)
+    for at in range(DIAGONALS):
+        for here, slots in turns(DIRS[at]):
+            @pl.when(here)
+            def _():
+                relay_copy(at, pl.ds(0, slots)).wait_recv()
+
+                def pass_on(slot, carry):
+                    onward_copy(at, pl.ds(slot, 1)).start()
+                    return carry
+
+                lax.fori_loop(0, slots, pass_on, 0)
     lax.fori_loop(EARLY, CAP, functools.partial(send_slot, False), 0)
 
     for at, step in enumerate(DIRS):
@@ -516,9 +521,10 @@
         plan_copy.start()
 
     for at in range(DIAGONALS):
-        @pl.when(turns(DIRS[at]))
-        def _():
-            onward_copy(at, pl.ds(0, RELAYED)).wait_send()
+        for here, slots in turns(DIRS[at]):
+            @pl.when(here)
+            def _():
+                onward_copy(at, pl.ds(0, slots)).wait_send()
     for at, way, here, share_of in passes:
         for thirds in range(1, planes):
             @pl.when(here & (share_of == thirds))
@@ -611,7 +617,7 @@
             pltpu.VMEM((BASES, DEGREE + 1, 8, side), jnp.float32),
             pltpu.VMEM(band_across.shape, jnp.bfloat16),
             pltpu.VMEM(band_down.shape, jnp.bfloat16),
-            pltpu.VMEM((DIAGONALS, RELAYED, block_side, block_side), jnp.bfloat16),
+            pltpu.VMEM((DIAGONALS, COLUMN_RELAYED, block_side, block_side), jnp.bfloat16),
             dma((9,)), dma, dma((count,)), dma((count,)), dma((count,)), dma((count,)),
             dma((count,)), dma((count,)), dma((DIAGONALS,)), dma((DIAGONALS,)),
             pltpu.VMEM((3 * DETOUR, block_side, block_side), jnp.bfloat16), dma, dma,

time: 40.4 us -> 40.6 us (level)
  no operation moved by 1% of the time
where the time goes in v10:
time: 40.6 us; the launch traced here: 40 us
  Pallas kernels  40 us (99%)
    pallas_call x1, Pallas kernels, on_device(): pl.pallas_call(send_kernel, out_shape=[jax.ShapeDtypeStruct((count + 1, C...  37.2 us
    pallas_call x1, Pallas kernels, on_device(): pl.pallas_call(join_kernel, out_shape=[jax.ShapeDtypeStruct((side, side),...  2.77 us

profile of v10, /device:TPU:105, one launch (start us, length us, event | category | flops | bytes accessed | tf_op | source)
XLA Modules:
  0.0 40.0 jit_solution(17251492873531023878)
XLA Ops:
  0.0 37.2 %send.1 = (bf16[9,16,128,128]{3,2,1,0:T(8,128)(2,1)S(1)}, s32[8,256]{1,0:T(8,128)S(4)}, f32[8,256]{1,0:T(8,128)S(4)}, f32[1024,1024]{1,0:T(8,128)S(1)}) custom-call(s32[1,64]{1,0:T(1,128)} %bitcast.2, s32[1,64]{1,0:T(1,128)} %bitcast.3, f32[3,15]{1,0:T(4,128)} %coef_hbm.1, bf16[64,128,128]{2,1,0:T(8,128)(2,1)} %pieces.1, bf16[1024,1024]{1,0:T(8,128)(2,1)} %template.1, ...), custom_call_target="tpu_custom_call" | custom-call | tf_op jit(solution)/shard_map/send/pallas_call | solution.py:590
  37.2 2.8 %join.1 = (f32[1024,1024]{1,0:T(8,128)}, f32[1024,1024]{1,0:T(8,128)S(1)}) custom-call(s32[8,256]{1,0:T(8,128)S(4)} %get-tuple-element.10.plan, f32[8,256]{1,0:T(8,128)S(4)} %get-tuple-element.11.share, bf16[9,16,128,128]{3,2,1,0:T(8,128)(2,1)S(1)} %get-tuple-element.12.arrived, ...), custom_call_target="tpu_custom_call", output_to_operand_aliasing={{1}: (3, {})} | custom-call | tf_op jit(solution)/shard_map/join/pallas_call | solution.py:638
